TPU v7x, 32 devices: a whole 2x2x4 slice. The times are simulated.
32 devices in a mesh: gx: 4 (over y, x), gy: 8 (over z, core).
Axes of the slice: x: 2, y: 2, z: 4, core: 2. Of those that a mesh axis runs over, the one named last changes fastest.
Arguments:
- component_concentration: float32 [64, 32, 3072], P(None, 'gx', 'gy'), may hold values from 0.3 to 3
- thermal_level: float32 [32, 3072], P('gx', 'gy'), may hold values from 0.7 to 2.5
- motion_vector: float32 [3, 32, 3072], P(None, 'gx', 'gy'), may hold values from -6 to 6
- component_weight_per_mole: float32 [64], replicated, may hold values from 0.3 to 3
- collision_size_third: float32 [64, 64], replicated, may hold values from 0.5 to 2
- potential_depth_volume: float32 [64, 64], replicated, may hold values from 0.5 to 4
- binary_drag_logpoly: float32 [4, 64, 64], replicated, may hold values from -0.15 to 2, as said below
- specific_warmth_intercept: float32 [64], replicated, may hold values from 3 to 8
- specific_warmth_gradient: float32 [64], replicated, may hold values from 0 to 1
- component_threshold_stress: float32 [64], replicated, may hold values from 0.5 to 2
Outputs:
- component_concentration_next: float32 [64, 32, 3072], P(None, 'gx', 'gy')
- motion_vector_next: float32 [3, 32, 3072], P(None, 'gx', 'gy')
- thermal_level_next: float32 [32, 3072], P('gx', 'gy')
- friction_limited_interval: float32 [], replicated
Inputs may be any that keep to these rules, and one draw needn't show every extreme that they name: `binary_drag_logpoly`: the first of the 4 coefficient matrices lies in 0.5 to 2, the others in -0.15 to 0.15.
All inputs are finite; a program needn't handle non-finite values.
Results may differ from a plain program's by a relative error of at most 0.0003.
Values sent between devices are 32-bit elements; how exact they have to be, the bound alone decides.
No kernel may reach another device: no remote copies, remote signals or barrier semaphores. Data moves between devices by JAX's collectives and lax.ppermute only.
A program may use at most 64 MiB of HBM per device.

v0:
```python
import jax
import jax.numpy as jnp
from jax import lax
from jax.sharding import PartitionSpec as P

LATERAL_ZONES = 16


HIGHEST = lax.Precision.HIGHEST
CFL_NUMBER = 0.12
GAS_SCALE = 0.01
BETA = 0.7862


def extended(value, sides, width):
    for axis, dim in sides:
        peers, length = (lax.axis_size(axis), value.shape[dim])
        up = [(i, (i + 1) % peers) for i in range(peers)]
        down = [(j, i) for i, j in up]
        last = lax.slice_in_dim(value, length - width, length, axis=dim)
        leading = lax.slice_in_dim(value, 0, width, axis=dim)
        before = lax.ppermute(last, axis, up)
        after = lax.ppermute(leading, axis, down)
        value = jnp.concatenate([before, value, after], axis=dim)
    return value


def mixture(fluid_snapshot, tables):
    (
        component_weight_per_mole,
        collision_size_third,
        potential_depth_volume,
        binary_drag_logpoly,
        specific_warmth_intercept,
        specific_warmth_gradient,
        component_threshold_stress,
    ) = tables
    species = component_weight_per_mole.shape[0]
    cell_shape = fluid_snapshot.shape[1:]
    flattened = fluid_snapshot.reshape(fluid_snapshot.shape[0], -1)
    partial_mass = flattened[:species]
    temper = flattened[species]
    mixture_density = jnp.sum(partial_mass, axis=0)
    fraction = partial_mass / mixture_density
    mole_count = fraction / component_weight_per_mole[:, None]
    mole_total = jnp.sum(mole_count, axis=0)
    molefr = mole_count / mole_total
    mean_mass = 1.0 / mole_total
    size_mix = jnp.sum(
        molefr
        * jnp.dot(
            collision_size_third, molefr, precision=HIGHEST, preferred_element_type=jnp.float32
        ),
        axis=0,
    )
    energy_mix = (
        jnp.sum(
            molefr
            * jnp.dot(
                potential_depth_volume,
                molefr,
                precision=HIGHEST,
                preferred_element_type=jnp.float32,
            ),
            axis=0,
        )
        / size_mix
    )
    reduced = temper / energy_mix
    collision = (
        1.16145 * reduced ** (-0.14874)
        + 0.52487 * jnp.exp(-0.7732 * reduced)
        + 2.16178 * jnp.exp(-2.43787 * reduced)
    )
    viscosity = (
        40.785
        * (0.809 * 0.809)
        * jnp.sqrt(mean_mass * temper)
        / (size_mix ** (2.0 / 3.0) * collision)
    )
    heat_molar = jnp.sum(
        molefr * (specific_warmth_intercept[:, None] + specific_warmth_gradient[:, None] * temper),
        axis=0,
    )
    excess = heat_molar - 2.5
    zeta_term = 2.0 + 10.5 * (reduced / 1.2593) ** 2
    psi_term = 1.0 + excess * (0.215 + 0.28288 * excess - 1.061 * BETA + 0.26665 * zeta_term) / (
        0.6366 + BETA * zeta_term + 1.061 * excess * BETA
    )
    conduct = 7.452 * viscosity * psi_term / mean_mass
    mass_heat_capacity = heat_molar / mean_mass
    pressure = GAS_SCALE * mixture_density * temper / mean_mass
    critical = jnp.sum(molefr * component_threshold_stress[:, None], axis=0)
    takahashi = 1.0 / (1.0 + 0.25 * (pressure / critical) ** 2)
    logtemp = jnp.log(temper)
    row_index = lax.broadcasted_iota(jnp.int32, (species, species), 0)
    col_index = lax.broadcasted_iota(jnp.int32, (species, species), 1)
    off_diagonal = jnp.where(row_index == col_index, 0.0, 1.0).astype(jnp.float32)
    resist = jnp.zeros_like(molefr)
    powers = jnp.ones_like(temper)
    for order in range(binary_drag_logpoly.shape[0]):
        resist = resist + powers * jnp.dot(
            binary_drag_logpoly[order] * off_diagonal,
            molefr,
            precision=HIGHEST,
            preferred_element_type=jnp.float32,
        )
        powers = powers * logtemp
    diffusive = takahashi * (1.0 - fraction) * temper * jnp.sqrt(temper) / (pressure * resist)
    carried = mixture_density * diffusive
    rate_max = jnp.maximum(
        jnp.maximum(viscosity / mixture_density, conduct / (mixture_density * mass_heat_capacity)),
        jnp.max(diffusive, axis=0),
    )
    packed = jnp.concatenate([carried, viscosity[None], conduct[None]], axis=0).reshape(
        (species + 2,) + cell_shape
    )
    return (packed, mass_heat_capacity.reshape(cell_shape), rate_max.reshape(cell_shape))


def z_shift(source, offset, z_cells):
    z_index = lax.broadcasted_iota(jnp.int32, (1, 1, source.shape[2]), 2) % z_cells
    shifted = jnp.roll(source, -offset, axis=2)
    if offset > 0:
        wrapped = jnp.roll(source, z_cells - offset, axis=2)
    else:
        wrapped = jnp.roll(source, -(offset + z_cells), axis=2)
    inside = (z_index + offset >= 0) & (z_index + offset < z_cells)
    return jnp.where(inside, shifted, wrapped)


def face_pair(source, axis_dim, cell_count, stride, z_cells):
    if stride > 0:
        pieces = [
            lax.slice_in_dim(
                source, offset * stride, (offset + cell_count + 1) * stride, axis=axis_dim
            )
            for offset in range(4)
        ]
    else:
        pieces = [
            z_shift(source, -1, z_cells),
            source,
            z_shift(source, 1, z_cells),
            z_shift(source, 2, z_cells),
        ]
    face_value = (9.0 * (pieces[1] + pieces[2]) - (pieces[0] + pieces[3])) / 16.0
    face_slope = (27.0 * (pieces[2] - pieces[1]) - (pieces[3] - pieces[0])) / 24.0
    return (face_value, face_slope)


def differ(through, axis_dim, cell_count, stride, z_cells):
    if stride > 0:
        return lax.slice_in_dim(
            through, stride, (cell_count + 1) * stride, axis=axis_dim
        ) - lax.slice_in_dim(through, 0, cell_count * stride, axis=axis_dim)
    return through - z_shift(through, -1, z_cells)


def line_rates(state_line, packed_line, axis_dim, cell_count, stride, z_cells):
    species = packed_line.shape[0] - 2
    partial_mass = state_line[:species]
    mixture_density = jnp.sum(partial_mass, axis=0, keepdims=True)
    fraction = partial_mass / mixture_density
    frac_value, frac_slope = face_pair(fraction, axis_dim, cell_count, stride, z_cells)
    carried_value = face_pair(packed_line[:species], axis_dim, cell_count, stride, z_cells)[0]
    drift = jnp.sum(carried_value * frac_slope, axis=0, keepdims=True)
    species_rate = differ(
        carried_value * frac_slope - frac_value * drift, axis_dim, cell_count, stride, z_cells
    )
    visc_value = face_pair(
        packed_line[species : species + 1], axis_dim, cell_count, stride, z_cells
    )[0]
    motion_slope = face_pair(state_line[species + 1 :], axis_dim, cell_count, stride, z_cells)[1]
    momentum = differ(visc_value * motion_slope, axis_dim, cell_count, stride, z_cells)
    cond_value = face_pair(packed_line[species + 1 :], axis_dim, cell_count, stride, z_cells)[0]
    temp_slope = face_pair(
        state_line[species : species + 1], axis_dim, cell_count, stride, z_cells
    )[1]
    thermal_power_source = differ(cond_value * temp_slope, axis_dim, cell_count, stride, z_cells)
    return (species_rate, momentum, thermal_power_source)


def edge_fix(wide):
    at_start = lax.axis_index("gx") == 0
    at_end = lax.axis_index("gx") == lax.axis_size("gx") - 1
    lower_rim = jnp.where(
        at_start, jnp.broadcast_to(wide[:, 2:3], wide[:, 0:2].shape), wide[:, 0:2]
    )
    upper_rim = jnp.where(
        at_end, jnp.broadcast_to(wide[:, -3:-2], wide[:, -2:].shape), wide[:, -2:]
    )
    return jnp.concatenate([lower_rim, wide[:, 2:-2], upper_rim], axis=1)


def body(
    component_concentration,
    thermal_level,
    motion_vector,
    component_weight_per_mole,
    collision_size_third,
    potential_depth_volume,
    binary_drag_logpoly,
    specific_warmth_intercept,
    specific_warmth_gradient,
    component_threshold_stress,
):
    tables = (
        component_weight_per_mole,
        collision_size_third,
        potential_depth_volume,
        binary_drag_logpoly,
        specific_warmth_intercept,
        specific_warmth_gradient,
        component_threshold_stress,
    )
    width_x = component_concentration.shape[1]
    z_cells = LATERAL_ZONES
    rows_y = component_concentration.shape[2] // z_cells
    pointwise_snapshot = jnp.concatenate(
        [component_concentration, thermal_level[None], motion_vector], axis=0
    )
    inner, mass_heat_capacity, rate_max = mixture(pointwise_snapshot, tables)
    fastest = lax.pmax(jnp.max(rate_max), ("gx", "gy"))
    friction_limited_interval = CFL_NUMBER / fastest
    wide_x = edge_fix(extended(pointwise_snapshot, (("gx", 1),), 2))
    wide_y = extended(pointwise_snapshot, (("gy", 2),), 2 * z_cells)
    packed_x = edge_fix(extended(inner, (("gx", 1),), 2))
    packed_y = extended(inner, (("gy", 2),), 2 * z_cells)
    x_part = line_rates(wide_x, packed_x, 1, width_x, 1, z_cells)
    y_part = line_rates(wide_y, packed_y, 2, rows_y, z_cells, z_cells)
    z_part = line_rates(pointwise_snapshot, inner, 2, z_cells, 0, z_cells)
    species_rate = x_part[0] + y_part[0] + z_part[0]
    momentum = x_part[1] + y_part[1] + z_part[1]
    thermal_power_source = x_part[2] + y_part[2] + z_part[2]
    mixture_density = jnp.sum(component_concentration, axis=0)
    component_concentration_next = (
        component_concentration + friction_limited_interval * species_rate
    )
    motion_vector_next = motion_vector + friction_limited_interval * (momentum / mixture_density)
    thermal_level_next = thermal_level + friction_limited_interval * (
        thermal_power_source[0] / (mixture_density * mass_heat_capacity)
    )
    return (
        component_concentration_next,
        motion_vector_next,
        thermal_level_next,
        friction_limited_interval,
    )


def solution(mesh):
    in_specs = (
        P(None, "gx", "gy"),
        P("gx", "gy"),
        P(None, "gx", "gy"),
        P(),
        P(),
        P(),
        P(),
        P(),
        P(),
        P(),
    )
    out_specs = (P(None, "gx", "gy"), P(None, "gx", "gy"), P("gx", "gy"), P())
    return jax.shard_map(body, mesh=mesh, in_specs=in_specs, out_specs=out_specs, check_vma=False)
```

profile of v0, /device:TPU:0, one launch (start us, length us, event | category | flops | bytes accessed | tf_op | source)
XLA Modules:
  0.0 109.0 jit_solution(13709355493654411625)
XLA Ops:
  0.7 1.3 %reduce_sum.113 = f32[8,384]{1,0:T(8,128)S(1)} reduce(f32[64,8,384]{2,1,0:T(8,128)} %param.10, f32[]{:T(128)} %constant.174.clone.1), dimensions={0}, to_apply=%region_0.0 | reduce | flops 193536 | bytes 798724 | tf_op jit(solution)/shard_map/reduce_sum | solution.py:43
  2.0 1.3 %fusion.30 = f32[8,384]{1,0:T(8,128)S(1)} fusion(f32[64,8,384]{2,1,0:T(8,128)} %param.10, f32[64]{0:T(128)} %param.13, f32[8,384]{1,0:T(8,128)S(1)} %reduce_sum.113), kind=kLoop, calls=%fused_computation.71 | loop fusion | flops 586752 | bytes 811264 | tf_op jit(solution)/shard_map/reduce_sum | solution.py:46
  5.1 0.8 convolution_multiply_fusion.2
  6.1 0.8 fusion
  6.9 2.0 %broadcast_multiply_fusion = (f32[64,3072]{1,0:T(8,128)}, f32[3072]{0:T(1024)S(1)}) fusion(f32[3072]{0:T(1024)S(1)} %div.244, f32[64,3072]{1,0:T(8,128)S(1)} %fusion, f32[64,3072]{1,0:T(8,128)S(1)} %bitcast.177, f32[4,64,64]{2,1,0:T(8,128)S(1)} %copy-done.17, f32[3072]{0:T(1024)S(1)} %get-tuple-element.87, f32[3072]{0:T(1024)S(1)} %get-tuple-element.90, ...), kind=kOutput, calls=%fused_computation.73 | convolution fusion | flops 153166848 | bytes 3264512 | tf_op jit(solution)/shard_map/dot_general | solution.py:102
  8.9 1.1 %fusion.10 = f32[3072]{0:T(1024)S(1)} fusion(f32[64,64]{1,0:T(8,128)S(1)} %copy-done, f32[64,3072]{1,0:T(8,128)S(1)} %bitcast.231, f32[3072]{0:T(1024)S(1)} %div.247, f32[64]{0:T(128)S(1)} %copy-done.23, f32[3072]{0:T(1024)S(1)} %div.244), kind=kOutput, calls=%fused_computation.25 | convolution fusion | flops 152564736 | bytes 839936 | tf_op jit(solution)/shard_map/dot_general | solution.py:51
  10.0 1.1 %fusion.11 = f32[3072]{0:T(1024)S(1)} fusion(f32[64,64]{1,0:T(8,128)S(1)} %copy-done.27, f32[64,3072]{1,0:T(8,128)S(1)} %bitcast.232, f32[3072]{0:T(1024)S(1)} %div.247, f32[64]{0:T(128)S(1)} %copy-done.23, f32[3072]{0:T(1024)S(1)} %div.244), kind=kOutput, calls=%fused_computation.26 | convolution fusion | flops 152564736 | bytes 839936 | tf_op jit(solution)/shard_map/dot_general | solution.py:59
  11.2 1.3 %copy.49 = f32[8,8,8,384]{3,2,1,0:T(8,128)S(1)} copy(f32[8,8,8,384]{3,1,2,0:T(8,128)} %bitcast.233) | data formatting | bytes 1572864
  13.2 0.9 fusion.142
  14.1 3.9 %collective-permute-start.1 = (f32[66,2,384]{2,1,0:T(2,128)}, f32[66,2,384]{2,1,0:T(2,128)}, u32[]{:S(2)}, u32[]{:S(2)}) collective-permute-start(f32[66,2,384]{2,1,0:T(2,128)} %get-tuple-element.29), channel_id=1, source_target_pairs={{8,0},{16,8},{24,16},{0,24},{9,1},{17,9},{25,17},{1,25},{10,2},{18... | collective-permute-start | bytes 608264 | tf_op jit(solution)/shard_map/ppermute | solution.py:23
  18.1 0.9 fusion.140
  19.0 2.9 %collective-permute-start.3 = (f32[68,2,384]{2,1,0:T(2,128)}, f32[68,2,384]{2,1,0:T(2,128)}, u32[]{:S(2)}, u32[]{:S(2)}) collective-permute-start(f32[68,2,384]{2,1,0:T(2,128)} %get-tuple-element.21), channel_id=1, source_target_pairs={{8,0},{16,8},{24,16},{0,24},{9,1},{17,9},{25,17},{1,25},{10,2},{18... | collective-permute-start | bytes 626696 | tf_op jit(solution)/shard_map/ppermute | solution.py:23
  21.9 0.9 fusion.143
  22.8 3.5 %collective-permute-start.5 = (f32[66,8,32]{2,1,0:T(8,128)}, f32[66,8,32]{2,1,0:T(8,128)}, u32[]{:S(2)}, u32[]{:S(2)}) collective-permute-start(f32[66,8,32]{2,1,0:T(8,128)} %get-tuple-element.33), channel_id=1, source_target_pairs={{1,0},{2,1},{3,2},{4,3},{5,4},{6,5},{7,6},{0,7},{9,8},{10,9},{11,1... | collective-permute-start | bytes 202760 | tf_op jit(solution)/shard_map/ppermute | solution.py:23
  28.8 0.9 fusion.141
  33.0 2.5 %fusion.133 = (f32[8,384]{1,0:T(8,128)S(1)}, f32[64,8,384]{2,1,0:T(8,128)S(1)}) fusion(f32[64,8,15]{2,1,0:T(8,128)S(1)} %get-tuple-element.48, f32[64,8,369]{2,1,0:T(8,128)S(1)} %get-tuple-element.50, f32[64,8,383]{2,1,0:T(8,128)S(1)} %get-tuple-element.44, f32[64,8,1]{2,1,0:T(8,128)S(1)} %get-tuple-element.46, f32[64,8,370]{2,1,0:T(8,128)S(1)} %bitcast.170, ...), kind=kLoop, calls=%fused_computation.291 | loop fusion | flops 5895168 | bytes 11809920 | tf_op jit(solution)/shard_map/reduce_sum | solution.py:167
  37.0 0.9 multiply_subtract_fusion.2
  38.7 37.9 %pmax.7 = f32[]{:T(128)} all-reduce(f32[]{:T(128)} %get-tuple-element.6), channel_id=1, replica_groups=mesh['gx'=4,'gy'=8] {'gx','gy'}, use_global_device_ids=true, to_apply=%region_8.9 | all-reduce | flops 1 | bytes 8 | tf_op jit(solution)/shard_map/pmax | solution.py:224
  78.6 1.1 %slice.841 = f32[64,8,369]{2,1,0:T(8,128)} slice(f32[64,8,384]{2,1,0:T(8,128)S(1)} %multiply_subtract_fusion.2), slice={[0:64], [0:8], [15:384]} | slice | bytes 1511424 | tf_op jit(solution)/shard_map/jit(_roll_static)/slice | solution.py:127
  79.7 0.9 slice.839
  82.1 3.5 %collective-permute-start.7 = (f32[68,8,32]{2,1,0:T(8,128)}, f32[68,8,32]{2,1,0:T(8,128)S(1)}, u32[]{:S(2)}, u32[]{:S(2)}) collective-permute-start(f32[68,8,32]{2,1,0:T(8,128)} %get-tuple-element.23), channel_id=1, source_target_pairs={{1,0},{2,1},{3,2},{4,3},{5,4},{6,5},{7,6},{0,7},{9,8},{10,9},{11,1... | collective-permute-start | bytes 208904 | tf_op jit(solution)/shard_map/ppermute | solution.py:23
  85.6 1.3 %maximum_maximum_fusion.1 = (f32[66,8,416]{2,1,0:T(8,128)S(1)}, f32[66,8,416]{2,1,0:T(8,128)S(1)}) fusion(f32[1,8,384]{2,1,0:T(8,128)S(1)} %bitcast.206, f32[1,8,384]{2,1,0:T(8,128)S(1)} %bitcast.222, f32[64,8,384]{2,1,0:T(8,128)S(1)} %bitcast.163, f32[66,8,32]{2,1,0:T(8,128)S(1)} %collective-permute-done.4, f32[66,8,32]{2,1,0:T(8,128)} %collective-permute-done.5), kind=kLoop, calls=%fused_computation.29 | loop fusion | flops 1317888 | bytes 2703360 | tf_op jit(solution)/shard_map/concatenate | solution.py:24
  87.0 0.8 fusion.83
  87.8 4.5 %collective-permute-done.6 = f32[68,8,32]{2,1,0:T(8,128)S(1)} collective-permute-done((f32[68,8,32]{2,1,0:T(8,128)}, f32[68,8,32]{2,1,0:T(8,128)S(1)}, u32[]{:S(2)}, u32[]{:S(2)}) %collective-permute-start.6) | collective-permute-done | bytes 69664 | tf_op jit(solution)/shard_map/ppermute | solution.py:22
  92.3 2.3 %collective-permute-start.2 = (f32[68,2,384]{2,1,0:T(2,128)S(1)}, f32[68,2,384]{2,1,0:T(2,128)S(1)}, u32[]{:S(2)}, u32[]{:S(2)}) collective-permute-start(f32[68,2,384]{2,1,0:T(2,128)S(1)} %copy-done.13), channel_id=1, source_target_pairs={{0,8},{8,16},{16,24},{24,0},{1,9},{9,17},{17,25},{25,1},{2,10},{10... | collective-permute-start | bytes 626696 | tf_op jit(solution)/shard_map/ppermute | solution.py:22
  95.4 1.4 %fusion.137 = (f32[8,400]{1,0:T(8,128)S(1)}, f32[64,8,400]{2,1,0:T(8,128)S(1)}) fusion(f32[64,8,448]{2,1,0:T(8,128)S(1)} %broadcast_divide_fusion, f32[66,8,416]{2,1,0:T(8,128)S(1)} %get-tuple-element.31, f32[66,8,416]{2,1,0:T(8,128)S(1)} %get-tuple-element.30), kind=kLoop, calls=%fused_computation.293 | loop fusion | flops 2454400 | bytes 7385600 | tf_op jit(solution)/shard_map/reduce_sum | solution.py:167
  96.9 0.9 multiply_subtract_fusion.1
  97.8 0.9 fusion.76
  98.8 1.1 broadcast_select_fusion.2
  100.9 1.0 broadcast_select_fusion
  102.9 1.1 %fusion.135 = (f32[9,384]{1,0:T(8,128)S(1)}, f32[64,9,384]{2,1,0:T(8,128)S(1)}) fusion(f32[64,12,384]{2,1,0:T(8,128)S(1)} %fusion.17, f32[66,10,384]{2,1,0:T(8,128)S(1)} %get-tuple-element.25, f32[66,10,384]{2,1,0:T(8,128)S(1)} %get-tuple-element.24), kind=kLoop, calls=%fused_computation.292 | loop fusion | flops 2650752 | bytes 7976448 | tf_op jit(solution)/shard_map/reduce_sum | solution.py:167
  106.3 1.6 %fusion.22 = f32[64,8,384]{2,1,0:T(8,128)} fusion(f32[64,8,384]{2,1,0:T(8,128)S(1)} %copy-done.1, f32[64,8,400]{2,1,0:T(8,128)S(1)} %multiply_subtract_fusion.1, f32[64,9,384]{2,1,0:T(8,128)S(1)} %multiply_subtract_fusion, f32[64,8,384]{2,1,0:T(8,128)S(1)} %multiply_subtract_fusion.2, f32[64,8,383]{2,1,0:T(8,128)S(1)} %bitcast.172, ...), kind=kLoop, calls=%fused_computation.51 | loop fusion | flops 1966080 | bytes 7078276 | tf_op jit(solution)/shard_map/add | solution.py:238
  (156 shorter events, 18.3 us)
Async XLA Ops:
  0.6 8.2 %copy-start = (f32[64,64]{1,0:T(8,128)S(1)}, f32[64,64]{1,0:T(8,128)}, u32[]{:S(2)}) copy-start(f32[64,64]{1,0:T(8,128)} %param.14) | copy-start | bytes 49156
  0.6 2.7 %copy-start.1 = (f32[64,8,384]{2,1,0:T(8,128)S(1)}, f32[64,8,384]{2,1,0:T(8,128)}, u32[]{:S(2)}) copy-start(f32[64,8,384]{2,1,0:T(8,128)} %param.10) | copy-start | bytes 2359300
  0.7 2.7 %copy-start.23 = (f32[64]{0:T(128)S(1)}, f32[64]{0:T(128)}, u32[]{:S(2)}) copy-start(f32[64]{0:T(128)} %param.13) | copy-start | bytes 772
  0.7 2.7 %copy-start.3 = (f32[8,384]{1,0:T(8,128)S(1)}, f32[8,384]{1,0:T(8,128)}, u32[]{:S(2)}) copy-start(f32[8,384]{1,0:T(8,128)} %param.11) | copy-start | bytes 36868
  0.7 2.7 %copy-start.26 = (f32[64]{0:T(128)S(1)}, f32[64]{0:T(128)}, u32[]{:S(2)}) copy-start(f32[64]{0:T(128)} %param.17) | copy-start | bytes 772
  0.7 2.7 %copy-start.25 = (f32[64]{0:T(128)S(1)}, f32[64]{0:T(128)}, u32[]{:S(2)}) copy-start(f32[64]{0:T(128)} %param.18) | copy-start | bytes 772
  0.7 2.7 %copy-start.24 = (f32[64]{0:T(128)S(1)}, f32[64]{0:T(128)}, u32[]{:S(2)}) copy-start(f32[64]{0:T(128)} %param.19) | copy-start | bytes 772
  3.4 0.9 copy-start.17
  3.8 8.7 %copy-start.15 = (f32[8,384]{1,0:T(8,128)}, f32[8,384]{1,0:T(8,128)S(1)}, u32[]{:S(2)}) copy-start(f32[8,384]{1,0:T(8,128)S(1)} %get-tuple-element.5) | copy-start | bytes 36868
  8.9 1.2 %copy-start.27 = (f32[64,64]{1,0:T(8,128)S(1)}, f32[64,64]{1,0:T(8,128)}, u32[]{:S(2)}) copy-start(f32[64,64]{1,0:T(8,128)} %param.15) | copy-start | bytes 49156
  12.5 5.5 %copy-start.2 = (f32[3,8,384]{2,1,0:T(8,128)S(1)}, f32[3,8,384]{2,1,0:T(8,128)}, u32[]{:S(2)}) copy-start(f32[3,8,384]{2,1,0:T(8,128)} %param.12) | copy-start | bytes 110596
  14.1 84.7 %collective-permute-start.1 = (f32[66,2,384]{2,1,0:T(2,128)}, f32[66,2,384]{2,1,0:T(2,128)}, u32[]{:S(2)}, u32[]{:S(2)}) collective-permute-start(f32[66,2,384]{2,1,0:T(2,128)} %get-tuple-element.29), channel_id=1, source_target_pairs={{8,0},{16,8},{24,16},{0,24},{9,1},{17,9},{25,17},{1,25},{10,2},{18... | collective-permute-start | bytes 608264 | tf_op jit(solution)/shard_map/ppermute | solution.py:23
  18.0 81.8 %collective-permute-start = (f32[66,2,384]{2,1,0:T(2,128)}, f32[66,2,384]{2,1,0:T(2,128)}, u32[]{:S(2)}, u32[]{:S(2)}) collective-permute-start(f32[66,2,384]{2,1,0:T(2,128)} %get-tuple-element.28), channel_id=1, source_target_pairs={{0,8},{8,16},{16,24},{24,0},{1,9},{9,17},{17,25},{25,1},{2,10},{10... | collective-permute-start | bytes 608264 | tf_op jit(solution)/shard_map/ppermute | solution.py:22
  19.0 81.4 %collective-permute-start.3 = (f32[68,2,384]{2,1,0:T(2,128)}, f32[68,2,384]{2,1,0:T(2,128)}, u32[]{:S(2)}, u32[]{:S(2)}) collective-permute-start(f32[68,2,384]{2,1,0:T(2,128)} %get-tuple-element.21), channel_id=1, source_target_pairs={{8,0},{16,8},{24,16},{0,24},{9,1},{17,9},{25,17},{1,25},{10,2},{18... | collective-permute-start | bytes 626696 | tf_op jit(solution)/shard_map/ppermute | solution.py:23
  22.8 59.2 %collective-permute-start.4 = (f32[66,8,32]{2,1,0:T(8,128)}, f32[66,8,32]{2,1,0:T(8,128)S(1)}, u32[]{:S(2)}, u32[]{:S(2)}) collective-permute-start(f32[66,8,32]{2,1,0:T(8,128)} %get-tuple-element.32), channel_id=1, source_target_pairs={{0,1},{1,2},{2,3},{3,4},{4,5},{5,6},{6,7},{7,0},{8,9},{9,10},{10,1... | collective-permute-start | bytes 202760 | tf_op jit(solution)/shard_map/ppermute | solution.py:22
  22.8 59.3 %collective-permute-start.5 = (f32[66,8,32]{2,1,0:T(8,128)}, f32[66,8,32]{2,1,0:T(8,128)}, u32[]{:S(2)}, u32[]{:S(2)}) collective-permute-start(f32[66,8,32]{2,1,0:T(8,128)} %get-tuple-element.33), channel_id=1, source_target_pairs={{1,0},{2,1},{3,2},{4,3},{5,4},{6,5},{7,6},{0,7},{9,8},{10,9},{11,1... | collective-permute-start | bytes 202760 | tf_op jit(solution)/shard_map/ppermute | solution.py:23
  27.2 10.8 %copy-start.11 = (f32[8,384]{1,0:T(8,128)}, f32[8,384]{1,0:T(8,128)S(1)}, u32[]{:S(2)}) copy-start(f32[8,384]{1,0:T(8,128)S(1)} %fusion.108) | copy-start | bytes 36868
  82.0 10.3 %collective-permute-start.6 = (f32[68,8,32]{2,1,0:T(8,128)}, f32[68,8,32]{2,1,0:T(8,128)S(1)}, u32[]{:S(2)}, u32[]{:S(2)}) collective-permute-start(f32[68,8,32]{2,1,0:T(8,128)} %get-tuple-element.22), channel_id=1, source_target_pairs={{0,1},{1,2},{2,3},{3,4},{4,5},{5,6},{6,7},{7,0},{8,9},{9,10},{10,1... | collective-permute-start | bytes 208904 | tf_op jit(solution)/shard_map/ppermute | solution.py:22
  82.1 10.2 %copy-start.13 = (f32[68,2,384]{2,1,0:T(2,128)S(1)}, f32[68,2,384]{2,1,0:T(2,128)}, u32[]{:S(2)}) copy-start(f32[68,2,384]{2,1,0:T(2,128)} %get-tuple-element.20) | copy-start | bytes 626692
  82.1 12.5 %collective-permute-start.7 = (f32[68,8,32]{2,1,0:T(8,128)}, f32[68,8,32]{2,1,0:T(8,128)S(1)}, u32[]{:S(2)}, u32[]{:S(2)}) collective-permute-start(f32[68,8,32]{2,1,0:T(8,128)} %get-tuple-element.23), channel_id=1, source_target_pairs={{1,0},{2,1},{3,2},{4,3},{5,4},{6,5},{7,6},{0,7},{9,8},{10,9},{11,1... | collective-permute-start | bytes 208904 | tf_op jit(solution)/shard_map/ppermute | solution.py:23
  92.3 9.6 %collective-permute-start.2 = (f32[68,2,384]{2,1,0:T(2,128)S(1)}, f32[68,2,384]{2,1,0:T(2,128)S(1)}, u32[]{:S(2)}, u32[]{:S(2)}) collective-permute-start(f32[68,2,384]{2,1,0:T(2,128)S(1)} %copy-done.13), channel_id=1, source_target_pairs={{0,8},{8,16},{16,24},{24,0},{1,9},{9,17},{17,25},{25,1},{2,10},{10... | collective-permute-start | bytes 626696 | tf_op jit(solution)/shard_map/ppermute | solution.py:22
  97.8 1.0 copy-start.8
  98.6 1.2 %copy-start.7 = (f32[66,384]{1,0:T(8,128)S(1)}, f32[66,384]{1,0:T(8,128)}, u32[]{:S(2)}) copy-start(f32[66,384]{1,0:T(8,128)} %get-tuple-element.95) | copy-start | bytes 304132
  100.0 0.9 copy-start.10
  100.0 2.0 %copy-start.9 = (f32[68,384]{1,0:T(8,128)S(1)}, f32[68,384]{1,0:T(8,128)}, u32[]{:S(2)}) copy-start(f32[68,384]{1,0:T(8,128)} %get-tuple-element.93) | copy-start | bytes 313348
  104.1 0.7 copy-start.12
  104.1 1.4 %copy-start.14 = (f32[3,8,369]{2,1,0:T(8,128)S(1)}, f32[3,8,369]{2,1,0:T(8,128)}, u32[]{:S(2)}) copy-start(f32[3,8,369]{2,1,0:T(8,128)} %slice.861) | copy-start | bytes 106276
  104.1 1.4 %copy-start.18 = (f32[3,8,1]{2,1,0:T(8,128)S(1)}, f32[3,8,1]{2,1,0:T(8,128)}, u32[]{:S(2)}) copy-start(f32[3,8,1]{2,1,0:T(8,128)} %slice.859) | copy-start | bytes 292
  104.2 1.4 %copy-start.19 = (f32[3,8,15]{2,1,0:T(8,128)S(1)}, f32[3,8,15]{2,1,0:T(8,128)}, u32[]{:S(2)}) copy-start(f32[3,8,15]{2,1,0:T(8,128)} %slice.862) | copy-start | bytes 4324
  104.2 2.1 %copy-start.4 = (f32[64,8,369]{2,1,0:T(8,128)S(1)}, f32[64,8,369]{2,1,0:T(8,128)}, u32[]{:S(2)}) copy-start(f32[64,8,369]{2,1,0:T(8,128)} %slice.841) | copy-start | bytes 2267140
  104.2 2.1 %copy-start.5 = (f32[64,8,1]{2,1,0:T(8,128)S(1)}, f32[64,8,1]{2,1,0:T(8,128)}, u32[]{:S(2)}) copy-start(f32[64,8,1]{2,1,0:T(8,128)} %slice.839) | copy-start | bytes 6148
  104.2 2.1 %copy-start.6 = (f32[64,8,15]{2,1,0:T(8,128)S(1)}, f32[64,8,15]{2,1,0:T(8,128)}, u32[]{:S(2)}) copy-start(f32[64,8,15]{2,1,0:T(8,128)} %slice.842) | copy-start | bytes 92164
  (4 other events, 2.9 us)
where the time goes:
time: 109 us
  blocking collectives  37.9 us (35%)
  other arithmetic  22.2 us (20%)
  local copies, waits for them, and re-layouts  18.2 us (17%)
  starting transfers between devices  16.2 us (15%)
  matrix products  6.64 us (6%)
  waiting for transfers between devices  4.54 us (4%)
  between operations  3.27 us (3%)
    pmax x1, blocking collectives, body(): fastest = lax.pmax(jnp.max(rate_max), ('gx', 'gy'))  37.9 us
    ppermute x4, starting transfers between devices, extended(): after = lax.ppermute(leading, axis, down)  13.9 us
    reduce_sum x3, other arithmetic, line_rates(): drift = jnp.sum(carried_value * frac_slope, axis=0, keepdims=True)  5.06 us
    ppermute x4, waiting for transfers between devices, extended(): before = lax.ppermute(last, axis, up)  4.53 us
    dot_general x4, matrix products, mixture(): jnp.dot(binary_drag_logpoly[order] * off_diagonal, molefr, precision=HIGH...  4.37 us
    unnamed x61, local copies, waits for them, and re-layouts  4.01 us
    slice x4, local copies, waits for them, and re-layouts, extended(): last = lax.slice_in_dim(value, length - width, length, axis=dim)  3.54 us
    slice x6, local copies, waits for them, and re-layouts, z_shift(): wrapped = jnp.roll(source, -(offset + z_cells), axis=2)  3.3 us
  transfers between devices with their start and end apart: 8, of which 1 were waited for; matrix products, arithmetic and copies ran while one was open for 25% of the time, Pallas kernels for 0%

commit v1 on v0

v1 whole, which is shorter than its diff:
```python
import functools

import jax
import jax.numpy as jnp
from jax import lax
from jax.experimental import pallas as pl
from jax.experimental.pallas import tpu as pltpu
from jax.sharding import PartitionSpec as P

LATERAL_ZONES = 16
CFL_NUMBER = 0.12
GAS_SCALE = 0.01
BETA = 0.7862
LANES = 128
EXTRA = 8
F32 = jnp.float32
VMEM = pltpu.MemorySpace.VMEM


def row_ids():
    return lax.broadcasted_iota(jnp.int32, (EXTRA, LANES), 0)


def lane_ids():
    return lax.broadcasted_iota(jnp.int32, (8, LANES), 1)


def split(value):
    high = value.astype(jnp.bfloat16)
    low = (value - high.astype(F32)).astype(jnp.bfloat16)
    return high, low


def fold_rows(value, op):
    parts = [value[8 * i : 8 * i + 8] for i in range(value.shape[0] // 8)]
    while len(parts) > 1:
        half = [op(parts[i], parts[i + 1]) for i in range(0, len(parts) - 1, 2)]
        parts = half + ([parts[-1]] if len(parts) % 2 else [])
    return parts[0]


def column_sum(value):
    return jnp.sum(fold_rows(value, jnp.add), axis=0, keepdims=True)


def write_matrix(mass_ref, size_ref, energy_ref, poly_ref, base_ref, slope_ref, crit_ref, mat_ref):
    species = mass_ref.shape[1]
    terms = poly_ref.shape[0] // species
    inverse = 1.0 / mass_ref[...]
    rows = lax.broadcasted_iota(jnp.int32, (species, species), 0)
    cols = lax.broadcasted_iota(jnp.int32, (species, species), 1)
    same = rows == cols
    column = jnp.sum(
        jnp.where(same, jnp.broadcast_to(inverse, (species, species)), 0.0), axis=1, keepdims=True
    )

    def put(start, block):
        high, low = split(block)
        high, low = high.astype(F32), low.astype(F32)
        mat_ref[start : start + block.shape[0], :] = jnp.concatenate(
            [high, high, low], axis=1
        ).astype(jnp.bfloat16)

    for k in range(terms):
        block = jnp.where(same, 0.0, poly_ref[k * species : (k + 1) * species, :])
        put(k * species, block * inverse)
    put(terms * species, size_ref[...] * inverse * column)
    put((terms + 1) * species, energy_ref[...] * inverse * column)
    lin = lax.broadcasted_iota(jnp.int32, (16, species), 0)
    block = jnp.where(lin == 0, 1.0, 0.0)
    for k, row in enumerate(
        (inverse, base_ref[...] * inverse, slope_ref[...] * inverse, crit_ref[...] * inverse)
    ):
        block = jnp.where(lin == k + 1, row, block)
    put((terms + 2) * species, block)


def mix_products(units, group, read, mat_ref, lin_ref, resist_ref, extra=None):
    ids = row_ids()

    def step(j, carry):
        pieces = [read(j, i) for i in range(group)]
        mass = [p[0] for p in pieces]
        species = mass[0].shape[0]
        terms = mat_ref.shape[0] // species - 2
        wide = jnp.concatenate(mass, axis=1)
        high, low = split(wide)
        stacked = jnp.concatenate([high, low, high], axis=0)
        product = jnp.dot(mat_ref[...], stacked, preferred_element_type=F32)
        for i, (m, temper) in enumerate(pieces):
            part = product[:, i * LANES : (i + 1) * LANES]
            u = j * group + i
            logt = jnp.log(temper)
            total = part[(terms - 1) * species : terms * species]
            for k in range(terms - 2, -1, -1):
                total = total * logt + part[k * species : (k + 1) * species]
            resist_ref[u, 0:species, :] = total
            size = column_sum(m * part[terms * species : (terms + 1) * species])
            energy = column_sum(m * part[(terms + 1) * species : (terms + 2) * species])
            lin = part[(terms + 2) * species : (terms + 2) * species + 8]
            lin = jnp.where(ids == 5, size, jnp.where(ids == 6, energy, lin))
            lin = jnp.where(ids == 7, temper, lin)
            lin_ref[pl.ds(pl.multiple_of(u * 8, 8), 8), :] = lin
            if extra is not None:
                extra(j, i, u, temper, part[(terms + 2) * species : (terms + 2) * species + 1])
        return carry

    lax.fori_loop(0, units // group, step, 0)


def mix_cells(units, lin_ref, plane_ref):
    def plane(k):
        return lin_ref[pl.ds(k, units, stride=8), :]

    density, moles, base, slope, crit, size, energy, temper = [plane(k) for k in range(8)]
    reduced = temper * size / energy
    collision = (
        1.16145 * jnp.exp(-0.14874 * jnp.log(reduced))
        + 0.52487 * jnp.exp(-0.7732 * reduced)
        + 2.16178 * jnp.exp(-2.43787 * reduced)
    )
    inv_moles = 1.0 / moles
    mean_mass = density * inv_moles
    size_mix = size * inv_moles * inv_moles
    viscosity = (
        (40.785 * (0.809 * 0.809))
        * jnp.sqrt(mean_mass * temper)
        / (jnp.exp((2.0 / 3.0) * jnp.log(size_mix)) * collision)
    )
    heat_total = base + slope * temper
    excess = heat_total * inv_moles - 2.5
    ratio = reduced * (1.0 / 1.2593)
    zeta = 2.0 + 10.5 * ratio * ratio
    psi = 1.0 + excess * (0.215 + 0.28288 * excess - 1.061 * BETA + 0.26665 * zeta) / (
        0.6366 + BETA * zeta + (1.061 * BETA) * excess
    )
    conduct = 7.452 * viscosity * psi / mean_mass
    over = GAS_SCALE * temper * moles * moles / crit
    takahashi = 1.0 / (1.0 + 0.25 * over * over)
    front = density * takahashi * jnp.sqrt(temper) * (1.0 / GAS_SCALE)
    inv_density = 1.0 / density
    inv_heat = 1.0 / heat_total
    plane_ref[0] = front
    plane_ref[1] = inv_density
    plane_ref[2] = viscosity
    plane_ref[3] = conduct
    plane_ref[4] = inv_heat
    return jnp.maximum(viscosity * inv_density, conduct * inv_heat)


def coefficient_rows(plane_ref, u):
    ids = row_ids()
    visc = plane_ref[2, pl.ds(u, 1), :]
    cond = plane_ref[3, pl.ds(u, 1), :]
    return jnp.where(ids == 0, cond, jnp.where(ids < 4, visc, 0.0))


def mix_halo(units, group, state_ref, mat_ref, lin_ref, plane_ref, carried_ref):
    species = state_ref.shape[1] - EXTRA

    def read(j, i):
        u = j * group + i
        density = state_ref[u, species + 4 : species + 5, :]
        return state_ref[u, 0:species, :] * density, state_ref[u, species : species + 1, :]

    mix_products(units, group, read, mat_ref, lin_ref, carried_ref)
    mix_cells(units, lin_ref, plane_ref)

    def step(u, carry):
        front = plane_ref[0, pl.ds(u, 1), :]
        fraction = state_ref[u, 0:species, :]
        carried_ref[u, 0:species, :] = front * ((1.0 - fraction) / carried_ref[u, 0:species, :])
        carried_ref[u, species : species + EXTRA, :] = coefficient_rows(plane_ref, u)
        return carry

    lax.fori_loop(0, units, step, 0)


def mixture_kernel(
    conc_hbm, temper_ref, motion_ref, mass_ref, size_ref, energy_ref, poly_ref, base_ref,
    slope_ref, crit_ref,
    state_ref, carried_ref, inverse_ref, mat_ref, first_x, second_x, first_y, second_y, rate_ref,
    conc_ref, lin_ref, plane_ref, other_ref, sem,
):
    tiles, _, _ = conc_ref.shape
    width = temper_ref.shape[0]
    species = mass_ref.shape[1]
    units = tiles * width
    copies = [
        pltpu.make_async_copy(
            conc_hbm.at[:, pl.ds(t * LANES, LANES)], conc_ref.at[t], sem.at[t]
        )
        for t in range(tiles)
    ]
    for c in copies:
        c.start()
    write_matrix(
        mass_ref, size_ref, energy_ref, poly_ref, base_ref, slope_ref, crit_ref, mat_ref
    )
    for t in range(tiles):
        ls = slice(t * LANES, (t + 1) * LANES)
        other_ref[t, 0:width, :] = temper_ref[:, ls]
        other_ref[t, width : 4 * width, :] = motion_ref[:, ls]
    for c in copies:
        c.wait()
    ids = row_ids()

    def read(x, t):
        mass = conc_ref[t, pl.ds(x, species, stride=width), :]
        return mass, other_ref[t, pl.ds(x, 1), :]

    def extra(x, t, u, temper, density):
        block = jnp.where(ids == 0, temper, jnp.where(ids == 4, density, 0.0))
        for c in range(3):
            row = other_ref[t, pl.ds((c + 1) * width + x, 1), :]
            block = jnp.where(ids == c + 1, row, block)
        state_ref[u, species : species + EXTRA, :] = block

    mix_products(units, tiles, read, mat_ref, lin_ref, carried_ref, extra)
    rates = mix_cells(units, lin_ref, plane_ref)

    def step(x, best):
        for t in range(tiles):
            u = x * tiles + t
            front = plane_ref[0, pl.ds(u, 1), :]
            inv_density = plane_ref[1, pl.ds(u, 1), :]
            fraction = conc_ref[t, pl.ds(x, species, stride=width), :] * inv_density
            share = (1.0 - fraction) / carried_ref[u, 0:species, :]
            state_ref[u, 0:species, :] = fraction
            carried_ref[u, 0:species, :] = front * share
            carried_ref[u, species : species + EXTRA, :] = coefficient_rows(plane_ref, u)
            inv_heat = plane_ref[4, pl.ds(u, 1), :]
            inverse_ref[u] = jnp.where(ids == 0, inv_heat, jnp.where(ids < 4, inv_density, 0.0))
            best = jnp.maximum(best, fold_rows(share, jnp.maximum) * (front * inv_density))
        return best

    best = lax.fori_loop(0, width, step, jnp.zeros((8, LANES), F32))
    top = jnp.maximum(jnp.max(best), jnp.max(rates))
    rate_ref[...] = jnp.full(rate_ref.shape, top, F32)

    even_x = lax.rem(lax.axis_index("gx"), 2) == 0
    upper = (width - 2) * tiles
    start_a = jnp.where(even_x, upper, 0)
    start_b = upper - start_a
    for k in range(2 * tiles):
        first_x[k] = state_ref[start_a + k]
        second_x[k] = state_ref[start_b + k]
    even_y = lax.rem(lax.axis_index("gy"), 2) == 0
    reach = 2 * LATERAL_ZONES
    per = LANES // reach
    lanes = lax.broadcasted_iota(jnp.int32, (species + EXTRA, LANES), 1)
    for g in range(width // per):
        low = high = None
        for k in range(per):
            x = g * per + k
            bottom = state_ref[x * tiles]
            ceiling = state_ref[x * tiles + tiles - 1]
            if k > 0:
                bottom = pltpu.roll(bottom, k * reach, 1)
            if k < per - 1:
                ceiling = pltpu.roll(ceiling, (k + 1) * reach, 1)
            if k == 0:
                low, high = bottom, ceiling
            else:
                low = jnp.where(lanes >= k * reach, bottom, low)
                high = jnp.where(lanes >= k * reach, ceiling, high)
        first_y[g] = jnp.where(even_y, high, low)
        second_y[g] = jnp.where(even_y, low, high)


def weigh(before, here, after, beyond):
    value = 9.0 * (here + after) - (before + beyond)
    slope = 27.0 * (after - here) - (beyond - before)
    return value, slope


def only_value(before, here, after, beyond):
    return 9.0 * (here + after) - (before + beyond)


def cross_kernel(
    state_ref, carried_ref, mat_ref, first_ref, second_ref,
    rate_ref,
    halo_ref, halo_carried, wrap_ref, wrap_carried, lin_ref, plane_ref, prod_ref, value_ref,
):
    units, rows, _ = state_ref.shape
    species = rows - EXTRA
    packs = first_ref.shape[0]
    zc = LATERAL_ZONES
    reach = 2 * zc
    per = LANES // reach
    width = packs * per
    tiles = units // width
    even_y = lax.rem(lax.axis_index("gy"), 2) == 0
    for g in range(packs):
        a, b = first_ref[g], second_ref[g]
        halo_ref[g] = jnp.where(even_y, a, b)
        halo_ref[packs + g] = jnp.where(even_y, b, a)
    mix_halo(2 * packs, 2 * packs, halo_ref, mat_ref, lin_ref, plane_ref, halo_carried)
    wide = lax.broadcasted_iota(jnp.int32, (rows, LANES), 1)
    for x in range(width):
        g, k = divmod(x, per)
        for src, dst in ((halo_ref, wrap_ref), (halo_carried, wrap_carried)):
            above, below = src[g], src[packs + g]
            if k > 0:
                above = pltpu.roll(above, LANES - k * reach, 1)
            if k < per - 1:
                below = pltpu.roll(below, LANES - (k + 1) * reach, 1)
            dst[x] = jnp.where(wide < LANES - reach, above, below)

    lane = lane_ids()
    chunks = rows // 8
    last = species // 8

    def y_shift(parts, amount):
        turned = [pltpu.roll(p, (LANES - amount) % LANES, 1) for p in parts]
        n = len(parts)
        if amount > 0:
            return [
                jnp.where(lane < LANES - amount, turned[t], turned[(t + 1) % n]) for t in range(n)
            ]
        return [jnp.where(lane >= -amount, turned[t], turned[t - 1]) for t in range(n)]

    z_index = lane % zc

    def z_shift(part, amount):
        near = pltpu.roll(part, (LANES - amount) % LANES, 1)
        far = pltpu.roll(part, (zc - amount) if amount > 0 else LANES - (zc + amount), 1)
        if amount > 0:
            return jnp.where(z_index < zc - amount, near, far)
        return jnp.where(z_index >= -amount, near, far)

    def step(x, carry):
        drift_y = [None] * (tiles + 1)
        drift_z = [None] * tiles
        for c in range(chunks):
            rs = slice(8 * c, 8 * c + 8)
            f = [state_ref[x * tiles + t, rs, :] for t in range(tiles)]
            h = [carried_ref[x * tiles + t, rs, :] for t in range(tiles)]
            fy, hy = f + [wrap_ref[x, rs, :]], h + [wrap_carried[x, rs, :]]
            fs = [y_shift(fy, a) for a in (-zc, zc, 2 * zc)]
            hs = [y_shift(hy, a) for a in (-zc, zc, 2 * zc)]
            for t in range(tiles + 1):
                v, s = weigh(fs[0][t], fy[t], fs[1][t], fs[2][t])
                p = only_value(hs[0][t], hy[t], hs[1][t], hs[2][t]) * s
                prod_ref[t, rs, :] = p
                value_ref[t, rs, :] = v
                if c < last:
                    drift_y[t] = p if c == 0 else drift_y[t] + p
            for t in range(tiles):
                v, s = weigh(z_shift(f[t], -1), f[t], z_shift(f[t], 1), z_shift(f[t], 2))
                p = only_value(z_shift(h[t], -1), h[t], z_shift(h[t], 1), z_shift(h[t], 2)) * s
                prod_ref[tiles + 1 + t, rs, :] = p
                value_ref[tiles + 1 + t, rs, :] = v
                if c < last:
                    drift_z[t] = p if c == 0 else drift_z[t] + p
        drift_y = [jnp.sum(d, axis=0, keepdims=True) * 0.0625 for d in drift_y]
        drift_z = [jnp.sum(d, axis=0, keepdims=True) * 0.0625 for d in drift_z]
        for c in range(chunks):
            rs = slice(8 * c, 8 * c + 8)

            def flux(slot, drift):
                p = prod_ref[slot, rs, :]
                return p - value_ref[slot, rs, :] * drift if c < last else p

            fy = [flux(t, drift_y[t]) for t in range(tiles + 1)]
            back = y_shift(fy, -zc)
            for t in range(tiles):
                fz = flux(tiles + 1 + t, drift_z[t])
                rate_ref[x * tiles + t, rs, :] = (fy[t] - back[t]) + (fz - z_shift(fz, -1))
        return carry

    lax.fori_loop(0, width, step, 0)


def stream_kernel(
    state_ref, carried_ref, mat_ref, first_ref, second_ref, partial_ref, inverse_ref,
    species_ref, others_ref,
    halo_ref, halo_carried, lin_ref, plane_ref,
):
    units, rows, _ = state_ref.shape
    species = rows - EXTRA
    half = first_ref.shape[0]
    tiles = half // 2
    width = units // tiles
    me, peers = lax.axis_index("gx"), lax.axis_size("gx")
    even_x = lax.rem(me, 2) == 0
    at_start, at_end = me == 0, me == peers - 1

    for k in range(half):
        a, b = first_ref[k], second_ref[k]
        low = jnp.where(even_x, b, a)
        high = jnp.where(even_x, a, b)
        halo_ref[k] = jnp.where(at_start, state_ref[k % tiles], low)
        halo_ref[half + k] = jnp.where(at_end, state_ref[units - tiles + k % tiles], high)
    mix_halo(2 * half, tiles, halo_ref, mat_ref, lin_ref, plane_ref, halo_carried)

    def step(t, carry):
        def row(inner, outer, x):
            if x < 0:
                return outer[(x + 2) * tiles + t]
            if x >= width:
                return outer[half + (x - width) * tiles + t]
            return inner[x * tiles + t]

        before = None
        for face in range(width + 1):
            f = [row(state_ref, halo_ref, face + k) for k in (-2, -1, 0, 1)]
            h = [row(carried_ref, halo_carried, face + k) for k in (-2, -1, 0, 1)]
            value, slope = weigh(*f)
            product = only_value(*h) * slope
            drift = column_sum(product[:species]) * 0.0625
            flux = jnp.concatenate(
                [product[:species] - value[:species] * drift, product[species:]], axis=0
            )
            if face > 0:
                x = face - 1
                u = x * tiles + t
                total = (flux - before) + partial_ref[u]
                species_ref[t, pl.ds(x, species, stride=width), :] = total[:species]
                others_ref[t, pl.ds(x, EXTRA, stride=width), :] = total[species:] * inverse_ref[u]
            before = flux
        return carry

    lax.fori_loop(0, tiles, step, 0)


def finish_kernel(
    conc_ref, temper_ref, motion_ref, species_ref, others_ref, top_ref,
    conc_out, temper_out, motion_out, interval_out,
):
    tiles = species_ref.shape[0]
    width = temper_ref.shape[0]
    fastest = jnp.max(top_ref[...], axis=0)
    interval = CFL_NUMBER / jnp.max(fastest, axis=(0, 1), keepdims=True)
    interval_out[...] = interval
    factor = interval * (1.0 / 384.0)
    for t in range(tiles):
        ls = slice(t * LANES, (t + 1) * LANES)
        conc_out[:, ls] = conc_ref[:, ls] + factor * species_ref[t]
        temper_out[:, ls] = temper_ref[:, ls] + factor * others_ref[t, 0:width, :]
        motion_out[:, ls] = motion_ref[:, ls] + factor * others_ref[t, width : 4 * width, :]


def call(kernel, name, outs, ins, scratch=()):
    return pl.pallas_call(
        kernel,
        out_shape=[jax.ShapeDtypeStruct(s, d) for s, d in outs],
        in_specs=[pl.BlockSpec(memory_space=m) for m in ins],
        out_specs=[pl.BlockSpec(memory_space=VMEM) for _ in outs],
        scratch_shapes=list(scratch),
        name=name,
    )


def body(
    component_concentration,
    thermal_level,
    motion_vector,
    component_weight_per_mole,
    collision_size_third,
    potential_depth_volume,
    binary_drag_logpoly,
    specific_warmth_intercept,
    specific_warmth_gradient,
    component_threshold_stress,
):
    species, width, line = component_concentration.shape
    terms = binary_drag_logpoly.shape[0]
    tiles = line // LANES
    units = width * tiles
    rows = species + EXTRA
    per = LANES // (2 * LATERAL_ZONES)
    packs = width // per
    nx, ny = lax.axis_size("gx"), lax.axis_size("gy")
    devices = nx * ny
    conc = component_concentration.reshape(species * width, line)
    motion = motion_vector.reshape(3 * width, line)
    mat_rows = (terms + 2) * species + 16
    mix_scratch = lambda n: [pltpu.VMEM((n * 8, LANES), F32), pltpu.VMEM((5, n, LANES), F32)]
    state, carried, inverse, mat, first_x, second_x, first_y, second_y, rate = call(
        mixture_kernel,
        "mixture",
        [
            ((units, rows, LANES), F32),
            ((units, rows, LANES), F32),
            ((units, EXTRA, LANES), F32),
            ((mat_rows, 3 * species), jnp.bfloat16),
            ((2 * tiles, rows, LANES), F32),
            ((2 * tiles, rows, LANES), F32),
            ((packs, rows, LANES), F32),
            ((packs, rows, LANES), F32),
            ((devices, 8, LANES), F32),
        ],
        [pl.ANY] + [VMEM] * 9,
        [pltpu.VMEM((tiles, species * width, LANES), F32)]
        + mix_scratch(units)
        + [pltpu.VMEM((tiles, 4 * width, LANES), F32)]
        + [pltpu.SemaphoreType.DMA((tiles,))],
    )(
        conc,
        thermal_level,
        motion,
        component_weight_per_mole[None],
        collision_size_third,
        potential_depth_volume,
        binary_drag_logpoly.reshape(terms * species, species),
        specific_warmth_intercept[None],
        specific_warmth_gradient[None],
        component_threshold_stress[None],
    )
    top = lax.all_to_all(rate, ("gx", "gy"), 0, 0, tiled=True)
    pair_first = lambda n: [(i, i ^ 1) for i in range(n)]
    pair_second = lambda n: [(i, (i + 1) % n if i % 2 else (i - 1) % n) for i in range(n)]
    inside = [(i, j) for i, j in pair_second(nx) if abs(i - j) == 1]
    got_first_x = lax.ppermute(first_x, "gx", pair_first(nx))
    got_second_x = lax.ppermute(second_x, "gx", inside)
    got_first_y = lax.ppermute(first_y, "gy", pair_first(ny))
    got_second_y = lax.ppermute(second_y, "gy", pair_second(ny))
    (cross,) = call(
        cross_kernel,
        "cross",
        [((units, rows, LANES), F32)],
        [VMEM] * 5,
        [
            pltpu.VMEM((2 * packs, rows, LANES), F32),
            pltpu.VMEM((2 * packs, rows, LANES), F32),
            pltpu.VMEM((width, rows, LANES), F32),
            pltpu.VMEM((width, rows, LANES), F32),
        ]
        + mix_scratch(2 * packs)
        + [pltpu.VMEM((2 * tiles + 1, rows, LANES), F32)] * 2,
    )(state, carried, mat, got_first_y, got_second_y)
    species_rate, other_rate = call(
        stream_kernel,
        "stream",
        [((tiles, species * width, LANES), F32), ((tiles, EXTRA * width, LANES), F32)],
        [VMEM] * 7,
        [
            pltpu.VMEM((4 * tiles, rows, LANES), F32),
            pltpu.VMEM((4 * tiles, rows, LANES), F32),
        ]
        + mix_scratch(4 * tiles),
    )(state, carried, mat, got_first_x, got_second_x, cross, inverse)
    conc_next, temper_next, motion_next, interval = call(
        finish_kernel,
        "finish",
        [
            (conc.shape, F32),
            (thermal_level.shape, F32),
            (motion.shape, F32),
            ((1, 1), F32),
        ],
        [VMEM] * 6,
    )(conc, thermal_level, motion, species_rate, other_rate, top)
    return (
        conc_next.reshape(component_concentration.shape),
        motion_next.reshape(motion_vector.shape),
        temper_next,
        interval.reshape(()),
    )


def solution(mesh):
    in_specs = (
        P(None, "gx", "gy"),
        P("gx", "gy"),
        P(None, "gx", "gy"),
    ) + (P(),) * 7
    out_specs = (P(None, "gx", "gy"), P(None, "gx", "gy"), P("gx", "gy"), P())
    return jax.shard_map(body, mesh=mesh, in_specs=in_specs, out_specs=out_specs, check_vma=False)
```

time: 109 us -> 43.5 us (0.40)
  the two profiles are of different devices: /device:TPU:0 before, /device:TPU:27 now
where the time goes in v1:
time: 43.5 us; the launch traced here: 43.2 us
  Pallas kernels  23.2 us (53%)
  starting transfers between devices  11.7 us (27%)
  waiting for transfers between devices  5.65 us (13%)
  local copies, waits for them, and re-layouts  2.01 us (5%)
  between operations  0.69 us (2%)
    pallas_call x1, Pallas kernels, body(): call(cross_kernel, 'cross', [((units, rows, LANES), F32)], [VMEM] * 5, [p...  9.19 us
    pallas_call x1, Pallas kernels, body(): call(mixture_kernel, 'mixture', [((units, rows, LANES), F32), ((units, ro...  6.37 us
    all_to_all x1, starting transfers between devices, body(): top = lax.all_to_all(rate, ('gx', 'gy'), 0, 0, tiled=True)  6.15 us
    pallas_call x1, Pallas kernels, body(): call(stream_kernel, 'stream', [((tiles, species * width, LANES), F32), ((...  5.04 us
    ppermute x1, waiting for transfers between devices, body(): got_second_y = lax.ppermute(second_y, 'gy', pair_second(ny))  4.66 us
    ppermute x1, starting transfers between devices, body(): got_second_x = lax.ppermute(second_x, 'gx', inside)  4.03 us
    pallas_call x1, Pallas kernels, body(): call(finish_kernel, 'finish', [(conc.shape, F32), (thermal_level.shape, F...  2.57 us
    unnamed x12, local copies, waits for them, and re-layouts  2.01 us
  transfers between devices with their start and end apart: 5, of which 2 were waited for; matrix products, arithmetic and copies ran while one was open for 0% of the time, Pallas kernels for 33%

profile of v1, /device:TPU:27, one launch (start us, length us, event | category | flops | bytes accessed | tf_op | source)
XLA Modules:
  0.0 43.2 jit_solution(7589546631186400082)
XLA Ops:
  0.6 6.4 %mixture.1 = (f32[24,72,128]{2,1,0:T(8,128)}, f32[24,72,128]{2,1,0:T(8,128)}, f32[24,8,128]{2,1,0:T(8,128)}, bf16[400,192]{1,0:T(8,128)(2,1)}, f32[6,72,128]{2,1...) custom-call(f32[512,384]{1,0:T(8,128)} %bitcast.10, ...), custom_call_target="tpu_custom_call" | custom-call | tf_op jit(solution)/shard_map/mixture/pallas_call | solution.py:481
  7.0 0.0 copy-start.5
  7.0 6.2 %all-to-all-start = ((f32[32,8,128]{2,1,0:T(8,128)}), f32[32,8,128]{2,1,0:T(8,128)S(1)}, u32[]{:S(2)}, u32[]{:S(2)}) async-start(f32[32,8,128]{2,1,0:T(8,128)} %get-tuple-element.29), calls=%async_computation | async-start | bytes 262144 | tf_op jit(solution)/shard_map/all_to_all | solution.py:512
  13.2 0.3 collective-permute-start
  13.5 0.0 copy-done.5
  13.5 4.0 %collective-permute-start.1 = (f32[6,72,128]{2,1,0:T(8,128)S(1)}, f32[6,72,128]{2,1,0:T(8,128)S(1)}, u32[]{:S(2)}, u32[]{:S(2)}) collective-permute-start(f32[6,72,128]{2,1,0:T(8,128)S(1)} %copy-done.5), channel_id=1, source_target_pairs={{8,16},{16,8},{9,17},{17,9},{10,18},{18,10},{11,19},{19,11},{12,20... | collective-permute-start | bytes 663560 | tf_op jit(solution)/shard_map/ppermute | solution.py:517
  17.6 1.0 %collective-permute-start.2 = (f32[2,72,128]{2,1,0:T(8,128)}, f32[2,72,128]{2,1,0:T(8,128)S(1)}, u32[]{:S(2)}, u32[]{:S(2)}) collective-permute-start(f32[2,72,128]{2,1,0:T(8,128)} %get-tuple-element.24), channel_id=1, source_target_pairs={{0,1},{1,0},{2,3},{3,2},{4,5},{5,4},{6,7},{7,6},{8,9},{9,8},{10,11... | collective-permute-start | bytes 221192 | tf_op jit(solution)/shard_map/ppermute | solution.py:518
  18.6 0.1 collective-permute-start.3
  18.7 1.0 %collective-permute-done.2.first_ref = f32[2,72,128]{2,1,0:T(8,128)S(1)} collective-permute-done((f32[2,72,128]{2,1,0:T(8,128)}, f32[2,72,128]{2,1,0:T(8,128)S(1)}, u32[]{:S(2)}, u32[]{:S(2)}) %collective-permute-start.2) | collective-permute-done | bytes 73760 | tf_op jit(solution)/shard_map/ppermute | solution.py:518
  19.7 0.0 copy-start.3
  19.7 4.7 %collective-permute-done.3.second_ref = f32[2,72,128]{2,1,0:T(8,128)S(1)} collective-permute-done((f32[2,72,128]{2,1,0:T(8,128)}, f32[2,72,128]{2,1,0:T(8,128)S(1)}, u32[]{:S(2)}, u32[]{:S(2)}) %collective-permute-start.3) | collective-permute-done | bytes 73760 | tf_op jit(solution)/shard_map/ppermute | solution.py:519
  24.4 0.0 copy-start.4
  24.4 0.0 copy-done.3
  24.4 0.6 %copy-done.4 = f32[2,72,128]{2,1,0:T(8,128)} copy-done((f32[2,72,128]{2,1,0:T(8,128)}, f32[2,72,128]{2,1,0:T(8,128)S(1)}, u32[]{:S(2)}) %copy-start.4) | copy-done | bytes 73752
  25.0 9.2 %cross.1.partial_ref = f32[24,72,128]{2,1,0:T(8,128)} custom-call(f32[24,72,128]{2,1,0:T(8,128)} %get-tuple-element.19.state_ref, f32[24,72,128]{2,1,0:T(8,128)} %get-tuple-element.20.carried_ref, bf16[400,192]{1,0:T(8,128)(2,1)} %get-tuple-element.21.mat_ref, f32[2,72,128]{2,1,0:T(8,128)} %copy-done.3, f32[2,72,128]{2,1,0:T(8,128)} %copy-done.4), custom_call_target="tpu_custom_call" | custom-call | tf_op jit(solution)/shard_map/cross/pallas_call | solution.py:520
  34.2 0.0 collective-permute-done.first_ref
  34.2 0.0 copy-start.1
  34.2 0.0 collective-permute-done.1.second_ref
  34.2 0.0 copy-start.2
  34.2 0.7 %copy-done.1 = f32[6,72,128]{2,1,0:T(8,128)} copy-done((f32[6,72,128]{2,1,0:T(8,128)}, f32[6,72,128]{2,1,0:T(8,128)S(1)}, u32[]{:S(2)}) %copy-start.1) | copy-done | bytes 221208
  34.9 0.1 copy-done.2
  34.9 5.0 %stream.1 = (f32[3,512,128]{2,1,0:T(8,128)}, f32[3,64,128]{2,1,0:T(8,128)}) custom-call(f32[24,72,128]{2,1,0:T(8,128)} %get-tuple-element.19.state_ref, f32[24,72,128]{2,1,0:T(8,128)} %get-tuple-element.20.carried_ref, bf16[400,192]{1,0:T(8,128)(2,1)} %get-tuple-element.21.mat_ref, f32[6,72,128]{2,1,0:T(8,128)} %copy-done.1, f32[6,72,128]{2,1,0:T(8,128)} %copy-done.2, ...), custom_call_target="tpu_custom_call" | custom-call | tf_op jit(solution)/shard_map/stream/pallas_call | solution.py:534
  40.0 0.0 all-to-all-done.top_ref
  40.0 0.0 copy-start
  40.0 0.6 %copy-done = f32[32,8,128]{2,1,0:T(8,128)} copy-done((f32[32,8,128]{2,1,0:T(8,128)}, f32[32,8,128]{2,1,0:T(8,128)S(1)}, u32[]{:S(2)}) %copy-start) | copy-done | bytes 131096
  40.6 2.6 %finish.1 = (f32[512,384]{1,0:T(8,128)}, f32[8,384]{1,0:T(8,128)}, f32[24,384]{1,0:T(8,128)}, f32[1,1]{1,0:T(1,128)}) custom-call(f32[512,384]{1,0:T(8,128)} %bitcast.11, f32[8,384]{1,0:T(8,128)} %temper_ref.3, f32[24,384]{1,0:T(8,128)} %bitcast.13, f32[3,512,128]{2,1,0:T(8,128)} %get-tuple-element.27.species_ref, ...), custom_call_target="tpu_custom_call" | custom-call | tf_op jit(solution)/shard_map/finish/pallas_call | solution.py:545
Async XLA Ops:
  7.0 6.5 %copy-start.5 = (f32[6,72,128]{2,1,0:T(8,128)S(1)}, f32[6,72,128]{2,1,0:T(8,128)}, u32[]{:S(2)}) copy-start(f32[6,72,128]{2,1,0:T(8,128)} %get-tuple-element.23) | copy-start | bytes 663556
  7.0 32.9 %all-to-all-start = ((f32[32,8,128]{2,1,0:T(8,128)}), f32[32,8,128]{2,1,0:T(8,128)S(1)}, u32[]{:S(2)}, u32[]{:S(2)}) async-start(f32[32,8,128]{2,1,0:T(8,128)} %get-tuple-element.29), calls=%async_computation | async-start | bytes 262144 | tf_op jit(solution)/shard_map/all_to_all | solution.py:512
  13.2 21.0 %collective-permute-start = (f32[6,72,128]{2,1,0:T(8,128)}, f32[6,72,128]{2,1,0:T(8,128)S(1)}, u32[]{:S(2)}, u32[]{:S(2)}) collective-permute-start(f32[6,72,128]{2,1,0:T(8,128)} %get-tuple-element.22), channel_id=1, source_target_pairs={{0,8},{8,0},{16,24},{24,16},{1,9},{9,1},{17,25},{25,17},{2,10},{10... | collective-permute-start | bytes 663560 | tf_op jit(solution)/shard_map/ppermute | solution.py:516
  13.5 20.7 %collective-permute-start.1 = (f32[6,72,128]{2,1,0:T(8,128)S(1)}, f32[6,72,128]{2,1,0:T(8,128)S(1)}, u32[]{:S(2)}, u32[]{:S(2)}) collective-permute-start(f32[6,72,128]{2,1,0:T(8,128)S(1)} %copy-done.5), channel_id=1, source_target_pairs={{8,16},{16,8},{9,17},{17,9},{10,18},{18,10},{11,19},{19,11},{12,20... | collective-permute-start | bytes 663560 | tf_op jit(solution)/shard_map/ppermute | solution.py:517
  17.6 2.1 %collective-permute-start.2 = (f32[2,72,128]{2,1,0:T(8,128)}, f32[2,72,128]{2,1,0:T(8,128)S(1)}, u32[]{:S(2)}, u32[]{:S(2)}) collective-permute-start(f32[2,72,128]{2,1,0:T(8,128)} %get-tuple-element.24), channel_id=1, source_target_pairs={{0,1},{1,0},{2,3},{3,2},{4,5},{5,4},{6,7},{7,6},{8,9},{9,8},{10,11... | collective-permute-start | bytes 221192 | tf_op jit(solution)/shard_map/ppermute | solution.py:518
  18.6 5.8 %collective-permute-start.3 = (f32[2,72,128]{2,1,0:T(8,128)}, f32[2,72,128]{2,1,0:T(8,128)S(1)}, u32[]{:S(2)}, u32[]{:S(2)}) collective-permute-start(f32[2,72,128]{2,1,0:T(8,128)} %get-tuple-element.25), channel_id=1, source_target_pairs={{0,7},{1,2},{2,1},{3,4},{4,3},{5,6},{6,5},{7,0},{8,15},{9,10},{10,... | collective-permute-start | bytes 221192 | tf_op jit(solution)/shard_map/ppermute | solution.py:519
  19.7 4.7 %copy-start.3 = (f32[2,72,128]{2,1,0:T(8,128)}, f32[2,72,128]{2,1,0:T(8,128)S(1)}, u32[]{:S(2)}) copy-start(f32[2,72,128]{2,1,0:T(8,128)S(1)} %collective-permute-done.2.first_ref) | copy-start | bytes 221188
  24.4 0.6 %copy-start.4 = (f32[2,72,128]{2,1,0:T(8,128)}, f32[2,72,128]{2,1,0:T(8,128)S(1)}, u32[]{:S(2)}) copy-start(f32[2,72,128]{2,1,0:T(8,128)S(1)} %collective-permute-done.3.second_ref) | copy-start | bytes 221188
  34.2 0.7 %copy-start.1 = (f32[6,72,128]{2,1,0:T(8,128)}, f32[6,72,128]{2,1,0:T(8,128)S(1)}, u32[]{:S(2)}) copy-start(f32[6,72,128]{2,1,0:T(8,128)S(1)} %collective-permute-done.first_ref) | copy-start | bytes 663556
  34.2 0.7 %copy-start.2 = (f32[6,72,128]{2,1,0:T(8,128)}, f32[6,72,128]{2,1,0:T(8,128)S(1)}, u32[]{:S(2)}) copy-start(f32[6,72,128]{2,1,0:T(8,128)S(1)} %collective-permute-done.1.second_ref) | copy-start | bytes 663556
  40.0 0.7 %copy-start = (f32[32,8,128]{2,1,0:T(8,128)}, f32[32,8,128]{2,1,0:T(8,128)S(1)}, u32[]{:S(2)}) copy-start(f32[32,8,128]{2,1,0:T(8,128)S(1)} %all-to-all-done.top_ref) | copy-start | bytes 393220

commit v2 on v1

--- a/solution.py
+++ b/solution.py
@@ -177,42 +177,51 @@
 
 
 def mixture_kernel(
-    conc_hbm, temper_ref, motion_ref, mass_ref, size_ref, energy_ref, poly_ref, base_ref,
-    slope_ref, crit_ref,
-    state_ref, carried_ref, inverse_ref, mat_ref, first_x, second_x, first_y, second_y, rate_ref,
-    conc_ref, lin_ref, plane_ref, other_ref, sem,
+    conc_hbm, temper_hbm, motion_hbm, mass_hbm, size_hbm, energy_hbm, poly_hbm, base_hbm,
+    slope_hbm, crit_hbm,
+    base_ref, state_ref, carried_ref, mat_ref, first_x, second_x, first_y, second_y, rate_ref,
+    mass_ref, size_ref, energy_ref, poly_ref, heat_ref, slope_ref, crit_ref, lin_ref, plane_ref,
+    table_sem, cell_sem,
 ):
-    tiles, _, _ = conc_ref.shape
-    width = temper_ref.shape[0]
+    tiles = base_ref.shape[0]
+    width = temper_hbm.shape[0]
     species = mass_ref.shape[1]
     units = tiles * width
-    copies = [
-        pltpu.make_async_copy(
-            conc_hbm.at[:, pl.ds(t * LANES, LANES)], conc_ref.at[t], sem.at[t]
-        )
-        for t in range(tiles)
+    cells = species * width
+    pairs = (
+        (mass_hbm, mass_ref), (size_hbm, size_ref), (energy_hbm, energy_ref),
+        (poly_hbm, poly_ref), (base_hbm, heat_ref), (slope_hbm, slope_ref), (crit_hbm, crit_ref),
+    )
+    tables = [
+        pltpu.make_async_copy(src, dst, table_sem.at[k]) for k, (src, dst) in enumerate(pairs)
     ]
-    for c in copies:
+    copies = []
+    for t in range(tiles):
+        ls = pl.ds(t * LANES, LANES)
+        for k, (src, start) in enumerate(
+            ((conc_hbm, 0), (temper_hbm, cells), (motion_hbm, cells + width))
+        ):
+            dst = base_ref.at[t, pl.ds(start, src.shape[0])]
+            copies.append(pltpu.make_async_copy(src.at[:, ls], dst, cell_sem.at[3 * t + k]))
+    for c in tables + copies:
         c.start()
+    for c in tables:
+        c.wait()
     write_matrix(
-        mass_ref, size_ref, energy_ref, poly_ref, base_ref, slope_ref, crit_ref, mat_ref
-    )
-    for t in range(tiles):
-        ls = slice(t * LANES, (t + 1) * LANES)
-        other_ref[t, 0:width, :] = temper_ref[:, ls]
-        other_ref[t, width : 4 * width, :] = motion_ref[:, ls]
+        mass_ref, size_ref, energy_ref, poly_ref, heat_ref, slope_ref, crit_ref, mat_ref
+    )
     for c in copies:
         c.wait()
     ids = row_ids()
 
     def read(x, t):
-        mass = conc_ref[t, pl.ds(x, species, stride=width), :]
-        return mass, other_ref[t, pl.ds(x, 1), :]
+        mass = base_ref[t, pl.ds(x, species, stride=width), :]
+        return mass, base_ref[t, pl.ds(cells + x, 1), :]
 
     def extra(x, t, u, temper, density):
         block = jnp.where(ids == 0, temper, jnp.where(ids == 4, density, 0.0))
         for c in range(3):
-            row = other_ref[t, pl.ds((c + 1) * width + x, 1), :]
+            row = base_ref[t, pl.ds(cells + (c + 1) * width + x, 1), :]
             block = jnp.where(ids == c + 1, row, block)
         state_ref[u, species : species + EXTRA, :] = block
 
@@ -224,13 +233,13 @@
             u = x * tiles + t
             front = plane_ref[0, pl.ds(u, 1), :]
             inv_density = plane_ref[1, pl.ds(u, 1), :]
-            fraction = conc_ref[t, pl.ds(x, species, stride=width), :] * inv_density
+            fraction = base_ref[t, pl.ds(x, species, stride=width), :] * inv_density
             share = (1.0 - fraction) / carried_ref[u, 0:species, :]
             state_ref[u, 0:species, :] = fraction
             carried_ref[u, 0:species, :] = front * share
             carried_ref[u, species : species + EXTRA, :] = coefficient_rows(plane_ref, u)
-            inv_heat = plane_ref[4, pl.ds(u, 1), :]
-            inverse_ref[u] = jnp.where(ids == 0, inv_heat, jnp.where(ids < 4, inv_density, 0.0))
+            state_ref[u, species + 5 : species + 6, :] = plane_ref[4, pl.ds(u, 1), :]
+            state_ref[u, species + 6 : species + 7, :] = inv_density
             best = jnp.maximum(best, fold_rows(share, jnp.maximum) * (front * inv_density))
         return best
 
@@ -278,11 +287,63 @@
     return 9.0 * (here + after) - (before + beyond)
 
 
+def z_shift(part, amount):
+    zc = LATERAL_ZONES
+    z_index = lax.broadcasted_iota(jnp.int32, part.shape, 1) % zc
+    near = pltpu.roll(part, (LANES - amount) % LANES, 1)
+    far = pltpu.roll(part, (zc - amount) if amount > 0 else LANES - (zc + amount), 1)
+    if amount > 0:
+        return jnp.where(z_index < zc - amount, near, far)
+    return jnp.where(z_index >= -amount, near, far)
+
+
+def span_kernel(group, state_ref, carried_ref, rate_ref, mat_ref):
+    units, rows, _ = state_ref.shape
+    species = rows - EXTRA
+    zc = LATERAL_ZONES
+    src = lax.broadcasted_iota(jnp.int32, (LANES, LANES), 0)
+    dst = lax.broadcasted_iota(jnp.int32, (LANES, LANES), 1)
+    near = (src // zc) == (dst // zc)
+    step = jnp.where(near, (src % zc - dst % zc + 1 + zc) % zc, 4)
+    value = jnp.where((step == 1) | (step == 2), 9.0, jnp.where((step == 0) | (step == 3), -1.0, 0.0))
+    slope = jnp.where(
+        step == 2,
+        27.0,
+        jnp.where(step == 1, -27.0, jnp.where(step == 3, -1.0, jnp.where(step == 0, 1.0, 0.0))),
+    )
+    for k in range(2):
+        rs = slice(k * LANES, (k + 1) * LANES)
+        mat_ref[rs, 0:LANES] = value.astype(jnp.bfloat16)
+        mat_ref[rs, LANES : 2 * LANES] = slope.astype(jnp.bfloat16)
+
+    def halves(ref, j):
+        wide = ref[pl.ds(j * group, group)].reshape(group * rows, LANES)
+        return jnp.concatenate(split(wide), axis=1)
+
+    def work(j, carry):
+        both = jnp.dot(halves(state_ref, j), mat_ref[...], preferred_element_type=F32)
+        front = jnp.dot(
+            halves(carried_ref, j), mat_ref[:, 0:LANES], preferred_element_type=F32
+        )
+        for i in range(group):
+            rs = slice(i * rows, (i + 1) * rows)
+            product = front[rs] * both[rs, LANES:]
+            drift = column_sum(product[:species]) * 0.0625
+            flux = jnp.concatenate(
+                [product[:species] - both[rs, :LANES][:species] * drift, product[species:]], axis=0
+            )
+            rate_ref[j * group + i] = flux - z_shift(flux, -1)
+        return carry
+
+    lax.fori_loop(0, units // group, work, 0)
+
+
 def cross_kernel(
-    state_ref, carried_ref, mat_ref, first_ref, second_ref,
-    rate_ref,
+    state_ref, carried_ref, mat_ref, first_ref, second_ref, partial_ref,
+    rate_ref, mat_out,
     halo_ref, halo_carried, wrap_ref, wrap_carried, lin_ref, plane_ref, prod_ref, value_ref,
 ):
+    mat_out[...] = mat_ref[...]
     units, rows, _ = state_ref.shape
     species = rows - EXTRA
     packs = first_ref.shape[0]
@@ -321,61 +382,40 @@
             ]
         return [jnp.where(lane >= -amount, turned[t], turned[t - 1]) for t in range(n)]
 
-    z_index = lane % zc
-
-    def z_shift(part, amount):
-        near = pltpu.roll(part, (LANES - amount) % LANES, 1)
-        far = pltpu.roll(part, (zc - amount) if amount > 0 else LANES - (zc + amount), 1)
-        if amount > 0:
-            return jnp.where(z_index < zc - amount, near, far)
-        return jnp.where(z_index >= -amount, near, far)
-
     def step(x, carry):
-        drift_y = [None] * (tiles + 1)
-        drift_z = [None] * tiles
+        drift = [None] * (tiles + 1)
         for c in range(chunks):
             rs = slice(8 * c, 8 * c + 8)
-            f = [state_ref[x * tiles + t, rs, :] for t in range(tiles)]
+            f = [state_ref[x * tiles + t, rs, :] for t in range(tiles)] + [wrap_ref[x, rs, :]]
             h = [carried_ref[x * tiles + t, rs, :] for t in range(tiles)]
-            fy, hy = f + [wrap_ref[x, rs, :]], h + [wrap_carried[x, rs, :]]
-            fs = [y_shift(fy, a) for a in (-zc, zc, 2 * zc)]
-            hs = [y_shift(hy, a) for a in (-zc, zc, 2 * zc)]
+            h = h + [wrap_carried[x, rs, :]]
+            fs = [y_shift(f, a) for a in (-zc, zc, 2 * zc)]
+            hs = [y_shift(h, a) for a in (-zc, zc, 2 * zc)]
             for t in range(tiles + 1):
-                v, s = weigh(fs[0][t], fy[t], fs[1][t], fs[2][t])
-                p = only_value(hs[0][t], hy[t], hs[1][t], hs[2][t]) * s
+                v, s = weigh(fs[0][t], f[t], fs[1][t], fs[2][t])
+                p = only_value(hs[0][t], h[t], hs[1][t], hs[2][t]) * s
                 prod_ref[t, rs, :] = p
                 value_ref[t, rs, :] = v
                 if c < last:
-                    drift_y[t] = p if c == 0 else drift_y[t] + p
-            for t in range(tiles):
-                v, s = weigh(z_shift(f[t], -1), f[t], z_shift(f[t], 1), z_shift(f[t], 2))
-                p = only_value(z_shift(h[t], -1), h[t], z_shift(h[t], 1), z_shift(h[t], 2)) * s
-                prod_ref[tiles + 1 + t, rs, :] = p
-                value_ref[tiles + 1 + t, rs, :] = v
-                if c < last:
-                    drift_z[t] = p if c == 0 else drift_z[t] + p
-        drift_y = [jnp.sum(d, axis=0, keepdims=True) * 0.0625 for d in drift_y]
-        drift_z = [jnp.sum(d, axis=0, keepdims=True) * 0.0625 for d in drift_z]
+                    drift[t] = p if c == 0 else drift[t] + p
+        drift = [jnp.sum(d, axis=0, keepdims=True) * 0.0625 for d in drift]
         for c in range(chunks):
             rs = slice(8 * c, 8 * c + 8)
-
-            def flux(slot, drift):
-                p = prod_ref[slot, rs, :]
-                return p - value_ref[slot, rs, :] * drift if c < last else p
-
-            fy = [flux(t, drift_y[t]) for t in range(tiles + 1)]
-            back = y_shift(fy, -zc)
+            flux = [prod_ref[t, rs, :] for t in range(tiles + 1)]
+            if c < last:
+                flux = [flux[t] - value_ref[t, rs, :] * drift[t] for t in range(tiles + 1)]
+            back = y_shift(flux, -zc)
             for t in range(tiles):
-                fz = flux(tiles + 1 + t, drift_z[t])
-                rate_ref[x * tiles + t, rs, :] = (fy[t] - back[t]) + (fz - z_shift(fz, -1))
+                u = x * tiles + t
+                rate_ref[u, rs, :] = partial_ref[u, rs, :] + (flux[t] - back[t])
         return carry
 
     lax.fori_loop(0, width, step, 0)
 
 
 def stream_kernel(
-    state_ref, carried_ref, mat_ref, first_ref, second_ref, partial_ref, inverse_ref,
-    species_ref, others_ref,
+    state_ref, carried_ref, mat_ref, first_ref, second_ref, partial_ref,
+    rate_ref,
     halo_ref, halo_carried, lin_ref, plane_ref,
 ):
     units, rows, _ = state_ref.shape
@@ -394,6 +434,8 @@
         halo_ref[k] = jnp.where(at_start, state_ref[k % tiles], low)
         halo_ref[half + k] = jnp.where(at_end, state_ref[units - tiles + k % tiles], high)
     mix_halo(2 * half, tiles, halo_ref, mat_ref, lin_ref, plane_ref, halo_carried)
+
+    ids = row_ids()
 
     def step(t, carry):
         def row(inner, outer, x):
@@ -417,8 +459,11 @@
                 x = face - 1
                 u = x * tiles + t
                 total = (flux - before) + partial_ref[u]
-                species_ref[t, pl.ds(x, species, stride=width), :] = total[:species]
-                others_ref[t, pl.ds(x, EXTRA, stride=width), :] = total[species:] * inverse_ref[u]
+                inv_heat = state_ref[u, species + 5 : species + 6, :]
+                inv_density = state_ref[u, species + 6 : species + 7, :]
+                factor = jnp.where(ids == 0, inv_heat, inv_density)
+                total = jnp.concatenate([total[:species], total[species:] * factor], axis=0)
+                rate_ref[t, pl.ds(x, rows, stride=width), :] = total
             before = flux
         return carry
 
@@ -426,31 +471,56 @@
 
 
 def finish_kernel(
-    conc_ref, temper_ref, motion_ref, species_ref, others_ref, top_ref,
-    conc_out, temper_out, motion_out, interval_out,
+    base_ref, rate_ref, top_ref,
+    conc_hbm, temper_hbm, motion_hbm, interval_ref,
+    next_ref, sem,
 ):
-    tiles = species_ref.shape[0]
-    width = temper_ref.shape[0]
+    tiles, count, _ = base_ref.shape
     fastest = jnp.max(top_ref[...], axis=0)
     interval = CFL_NUMBER / jnp.max(fastest, axis=(0, 1), keepdims=True)
-    interval_out[...] = interval
+    interval_ref[...] = interval
     factor = interval * (1.0 / 384.0)
+    copies = []
     for t in range(tiles):
-        ls = slice(t * LANES, (t + 1) * LANES)
-        conc_out[:, ls] = conc_ref[:, ls] + factor * species_ref[t]
-        temper_out[:, ls] = temper_ref[:, ls] + factor * others_ref[t, 0:width, :]
-        motion_out[:, ls] = motion_ref[:, ls] + factor * others_ref[t, width : 4 * width, :]
+        next_ref[t] = base_ref[t] + factor * rate_ref[t, 0:count, :]
+        ls = pl.ds(t * LANES, LANES)
+        start = 0
+        for k, dst in enumerate((conc_hbm, temper_hbm, motion_hbm)):
+            src = next_ref.at[t, pl.ds(start, dst.shape[0])]
+            copy = pltpu.make_async_copy(src, dst.at[:, ls], sem.at[3 * t + k])
+            copy.start()
+            copies.append(copy)
+            start += dst.shape[0]
+    for copy in copies:
+        copy.wait()
 
 
 def call(kernel, name, outs, ins, scratch=()):
-    return pl.pallas_call(
+    shapes, specs = [], []
+    for shape, dtype, place in outs:
+        shapes.append(
+            pltpu.VMEM(shape, dtype) if place is True else jax.ShapeDtypeStruct(shape, dtype)
+        )
+        specs.append(pl.BlockSpec(memory_space=pl.ANY if place is pl.ANY else VMEM))
+    run = pl.pallas_call(
         kernel,
-        out_shape=[jax.ShapeDtypeStruct(s, d) for s, d in outs],
-        in_specs=[pl.BlockSpec(memory_space=m) for m in ins],
-        out_specs=[pl.BlockSpec(memory_space=VMEM) for _ in outs],
+        out_shape=shapes,
+        in_specs=[pl.BlockSpec(memory_space=pltpu.HBM if m is pl.ANY else VMEM) for m in ins],
+        out_specs=specs,
         scratch_shapes=list(scratch),
         name=name,
-    )
+        compiler_params=pltpu.CompilerParams(vmem_limit_bytes=16 << 20),
+    )
+
+    def apply(*args):
+        return run(
+            *[
+                pltpu.with_memory_space_constraint(a, pltpu.VMEM if m is True else pltpu.HBM)
+                for a, m in zip(args, ins)
+            ]
+        )
+
+    return apply
 
 
 def body(
@@ -477,26 +547,36 @@
     conc = component_concentration.reshape(species * width, line)
     motion = motion_vector.reshape(3 * width, line)
     mat_rows = (terms + 2) * species + 16
+    count = (species + 4) * width
+    keep = True
+    field = ((units, rows, LANES), F32, keep)
     mix_scratch = lambda n: [pltpu.VMEM((n * 8, LANES), F32), pltpu.VMEM((5, n, LANES), F32)]
-    state, carried, inverse, mat, first_x, second_x, first_y, second_y, rate = call(
+    base, state, carried, mat, first_x, second_x, first_y, second_y, rate = call(
         mixture_kernel,
         "mixture",
         [
-            ((units, rows, LANES), F32),
-            ((units, rows, LANES), F32),
-            ((units, EXTRA, LANES), F32),
-            ((mat_rows, 3 * species), jnp.bfloat16),
-            ((2 * tiles, rows, LANES), F32),
-            ((2 * tiles, rows, LANES), F32),
-            ((packs, rows, LANES), F32),
-            ((packs, rows, LANES), F32),
-            ((devices, 8, LANES), F32),
+            ((tiles, count, LANES), F32, keep),
+            field,
+            field,
+            ((mat_rows, 3 * species), jnp.bfloat16, keep),
+            ((2 * tiles, rows, LANES), F32, keep),
+            ((2 * tiles, rows, LANES), F32, keep),
+            ((packs, rows, LANES), F32, keep),
+            ((packs, rows, LANES), F32, keep),
+            ((devices, 8, LANES), F32, keep),
         ],
-        [pl.ANY] + [VMEM] * 9,
-        [pltpu.VMEM((tiles, species * width, LANES), F32)]
+        [pl.ANY] * 10,
+        [
+            pltpu.VMEM((1, species), F32),
+            pltpu.VMEM((species, species), F32),
+            pltpu.VMEM((species, species), F32),
+            pltpu.VMEM((terms * species, species), F32),
+            pltpu.VMEM((1, species), F32),
+            pltpu.VMEM((1, species), F32),
+            pltpu.VMEM((1, species), F32),
+        ]
         + mix_scratch(units)
-        + [pltpu.VMEM((tiles, 4 * width, LANES), F32)]
-        + [pltpu.SemaphoreType.DMA((tiles,))],
+        + [pltpu.SemaphoreType.DMA((7,)), pltpu.SemaphoreType.DMA((3 * tiles,))],
     )(
         conc,
         thermal_level,
@@ -517,11 +597,19 @@
     got_second_x = lax.ppermute(second_x, "gx", inside)
     got_first_y = lax.ppermute(first_y, "gy", pair_first(ny))
     got_second_y = lax.ppermute(second_y, "gy", pair_second(ny))
-    (cross,) = call(
+    group = 2 * tiles if width % 2 == 0 else tiles
+    (span,) = call(
+        functools.partial(span_kernel, group),
+        "span",
+        [field],
+        [keep] * 2,
+        [pltpu.VMEM((2 * LANES, 2 * LANES), jnp.bfloat16)],
+    )(state, carried)
+    cross, mat = call(
         cross_kernel,
         "cross",
-        [((units, rows, LANES), F32)],
-        [VMEM] * 5,
+        [field, ((mat_rows, 3 * species), jnp.bfloat16, keep)],
+        [keep] * 6,
         [
             pltpu.VMEM((2 * packs, rows, LANES), F32),
             pltpu.VMEM((2 * packs, rows, LANES), F32),
@@ -529,30 +617,31 @@
             pltpu.VMEM((width, rows, LANES), F32),
         ]
         + mix_scratch(2 * packs)
-        + [pltpu.VMEM((2 * tiles + 1, rows, LANES), F32)] * 2,
-    )(state, carried, mat, got_first_y, got_second_y)
-    species_rate, other_rate = call(
+        + [pltpu.VMEM((tiles + 1, rows, LANES), F32)] * 2,
+    )(state, carried, mat, got_first_y, got_second_y, span)
+    (total,) = call(
         stream_kernel,
         "stream",
-        [((tiles, species * width, LANES), F32), ((tiles, EXTRA * width, LANES), F32)],
-        [VMEM] * 7,
+        [((tiles, rows * width, LANES), F32, keep)],
+        [keep] * 6,
         [
             pltpu.VMEM((4 * tiles, rows, LANES), F32),
             pltpu.VMEM((4 * tiles, rows, LANES), F32),
         ]
         + mix_scratch(4 * tiles),
-    )(state, carried, mat, got_first_x, got_second_x, cross, inverse)
+    )(state, carried, mat, got_first_x, got_second_x, cross)
     conc_next, temper_next, motion_next, interval = call(
         finish_kernel,
         "finish",
         [
-            (conc.shape, F32),
-            (thermal_level.shape, F32),
-            (motion.shape, F32),
-            ((1, 1), F32),
+            (conc.shape, F32, pl.ANY),
+            (thermal_level.shape, F32, pl.ANY),
+            (motion.shape, F32, pl.ANY),
+            ((1, 1), F32, None),
         ],
-        [VMEM] * 6,
-    )(conc, thermal_level, motion, species_rate, other_rate, top)
+        [keep] * 3,
+        [pltpu.VMEM((tiles, count, LANES), F32), pltpu.SemaphoreType.DMA((3 * tiles,))],
+    )(base, total, top)
     return (
         conc_next.reshape(component_concentration.shape),
         motion_next.reshape(motion_vector.shape),

time: 43.5 us -> 31.8 us (0.73)
  Pallas kernels: 23.2 us -> 15.3 us
  local copies, waits for them, and re-layouts: 2.01 us -> 0 us
  waiting for transfers between devices: 5.65 us -> 3.83 us
    pallas_call x4 -> x5, Pallas kernels: 23.2 us -> 15.3 us  [apply(): run(*[pltpu.with_memory_space_constraint(a, pltpu.VMEM if m is True else...]
    unnamed x12 -> x0, local copies, waits for them, and re-layouts: 2.01 us -> none
    ppermute x1, waiting for transfers between devices: 0.98 us -> 0.01 us  [body(): got_first_y = lax.ppermute(first_y, 'gy', pair_first(ny))]
    ppermute x1, waiting for transfers between devices: 4.66 us -> 3.81 us  [body(): got_second_y = lax.ppermute(second_y, 'gy', pair_second(ny))]
  transfers between devices with their start and end apart: 5 -> 5, of which waited for: 2 -> 1; matrix products, arithmetic and copies ran while one was open for 0% -> 0% of each run, Pallas kernels for 33% -> 24%
where the time goes in v2:
time: 31.8 us; the launch traced here: 31.6 us
  Pallas kernels  15.3 us (48%)
  starting transfers between devices  11.7 us (37%)
  waiting for transfers between devices  3.83 us (12%)
  between operations  0.72 us (2%)
    pallas_call x5, Pallas kernels, apply(): run(*[pltpu.with_memory_space_constraint(a, pltpu.VMEM if m is True else...  15.3 us
    all_to_all x1, starting transfers between devices, body(): top = lax.all_to_all(rate, ('gx', 'gy'), 0, 0, tiled=True)  6.19 us
    ppermute x1, starting transfers between devices, body(): got_second_x = lax.ppermute(second_x, 'gx', inside)  4.03 us
    ppermute x1, waiting for transfers between devices, body(): got_second_y = lax.ppermute(second_y, 'gy', pair_second(ny))  3.81 us
    ppermute x1, starting transfers between devices, body(): got_first_y = lax.ppermute(first_y, 'gy', pair_first(ny))  1.01 us
  transfers between devices with their start and end apart: 5, of which 1 were waited for; matrix products, arithmetic and copies ran while one was open for 0% of the time, Pallas kernels for 24%

profile of v2, /device:TPU:27, one launch (start us, length us, event | category | flops | bytes accessed | tf_op | source)
XLA Modules:
  0.0 31.6 jit_solution(4725347112063266092)
XLA Ops:
  0.6 5.0 %mixture.1 = (f32[3,544,128]{2,1,0:T(8,128)S(1)}, f32[24,72,128]{2,1,0:T(8,128)S(1)}, f32[24,72,128]{2,1,0:T(8,128)S(1)}, bf16[400,192]{1,0:T(8,128)(2,1)S(1)}, ...) custom-call(f32[512,384]{1,0:T(8,128)} %bitcast.10, ...), custom_call_target="tpu_custom_call" | custom-call | tf_op jit(solution)/shard_map/mixture/pallas_call | solution.py:516
  5.7 6.2 %all-to-all-start = ((f32[32,8,128]{2,1,0:T(8,128)}), f32[32,8,128]{2,1,0:T(8,128)}, u32[]{:S(2)}, u32[]{:S(2)}) async-start(f32[32,8,128]{2,1,0:T(8,128)} %get-tuple-element.29), calls=%async_computation | async-start | bytes 262144 | tf_op jit(solution)/shard_map/all_to_all | solution.py:592
  11.9 0.3 %collective-permute-start.2 = (f32[6,72,128]{2,1,0:T(8,128)S(1)}, f32[6,72,128]{2,1,0:T(8,128)S(1)}, u32[]{:S(2)}, u32[]{:S(2)}) collective-permute-start(f32[6,72,128]{2,1,0:T(8,128)S(1)} %get-tuple-element.26), channel_id=1, source_target_pairs={{0,8},{8,0},{16,24},{24,16},{1,9},{9,1},{17,25},{25,17},{2,10},{10... | collective-permute-start | bytes 663560 | tf_op jit(solution)/shard_map/ppermute | solution.py:596
  12.2 4.0 %collective-permute-start.3 = (f32[6,72,128]{2,1,0:T(8,128)S(1)}, f32[6,72,128]{2,1,0:T(8,128)S(1)}, u32[]{:S(2)}, u32[]{:S(2)}) collective-permute-start(f32[6,72,128]{2,1,0:T(8,128)S(1)} %get-tuple-element.27), channel_id=1, source_target_pairs={{8,16},{16,8},{9,17},{17,9},{10,18},{18,10},{11,19},{19,11},{12,20... | collective-permute-start | bytes 663560 | tf_op jit(solution)/shard_map/ppermute | solution.py:597
  16.2 1.0 %collective-permute-start = (f32[2,72,128]{2,1,0:T(8,128)S(1)}, f32[2,72,128]{2,1,0:T(8,128)S(1)}, u32[]{:S(2)}, u32[]{:S(2)}) collective-permute-start(f32[2,72,128]{2,1,0:T(8,128)S(1)} %get-tuple-element.23), channel_id=1, source_target_pairs={{0,1},{1,0},{2,3},{3,2},{4,5},{5,4},{6,7},{7,6},{8,9},{9,8},{10,11... | collective-permute-start | bytes 221192 | tf_op jit(solution)/shard_map/ppermute | solution.py:598
  17.2 0.1 collective-permute-start.1
  17.4 1.6 %span.1.partial_ref = f32[24,72,128]{2,1,0:T(8,128)S(1)} custom-call(f32[24,72,128]{2,1,0:T(8,128)S(1)} %get-tuple-element.20.state_ref, f32[24,72,128]{2,1,0:T(8,128)S(1)} %get-tuple-element.21.carried_ref), custom_call_target="tpu_custom_call" | custom-call | tf_op jit(solution)/shard_map/span/pallas_call | solution.py:516
  19.0 0.0 collective-permute-done.first_ref
  19.0 3.8 %collective-permute-done.1.second_ref = f32[2,72,128]{2,1,0:T(8,128)S(1)} collective-permute-done((f32[2,72,128]{2,1,0:T(8,128)S(1)}, f32[2,72,128]{2,1,0:T(8,128)S(1)}, u32[]{:S(2)}, u32[]{:S(2)}) %collective-permute-start.1) | collective-permute-done | bytes 73760 | tf_op jit(solution)/shard_map/ppermute | solution.py:599
  22.8 3.9 %cross.1 = (f32[24,72,128]{2,1,0:T(8,128)S(1)}, bf16[400,192]{1,0:T(8,128)(2,1)S(1)}) custom-call(f32[24,72,128]{2,1,0:T(8,128)S(1)} %get-tuple-element.20.state_ref, f32[24,72,128]{2,1,0:T(8,128)S(1)} %get-tuple-element.21.carried_ref, bf16[400,192]{1,0:T(8,128)(2,1)S(1)} %get-tuple-element.22.mat_ref, f32[2,72,128]{2,1,0:T(8,128)S(1)} %collective-permute-done.first_ref, ...), custom_call_target="tpu_custom_call" | custom-call | tf_op jit(solution)/shard_map/cross/pallas_call | solution.py:516
  26.7 0.0 collective-permute-done.2.first_ref
  26.7 0.0 collective-permute-done.3.second_ref
  26.8 2.2 %stream.1.rate_ref = f32[3,576,128]{2,1,0:T(8,128)S(1)} custom-call(f32[24,72,128]{2,1,0:T(8,128)S(1)} %get-tuple-element.20.state_ref, f32[24,72,128]{2,1,0:T(8,128)S(1)} %get-tuple-element.21.carried_ref, bf16[400,192]{1,0:T(8,128)(2,1)S(1)} %get-tuple-element.25.mat_ref, f32[6,72,128]{2,1,0:T(8,128)S(1)} %collective-permute-done.2.first_ref, ...), custom_call_target="tpu_custom_call" | custom-call | tf_op jit(solution)/shard_map/stream/pallas_call | solution.py:516
  29.0 0.0 all-to-all-done.top_ref
  29.0 2.6 %finish.1 = (f32[512,384]{1,0:T(8,128)}, f32[8,384]{1,0:T(8,128)}, f32[24,384]{1,0:T(8,128)}, f32[1,1]{1,0:T(1,128)}) custom-call(f32[3,544,128]{2,1,0:T(8,128)S(1)} %get-tuple-element.19.base_ref, f32[3,576,128]{2,1,0:T(8,128)S(1)} %stream.1.rate_ref, f32[32,8,128]{2,1,0:T(8,128)} %all-to-all-done.top_ref), custom_call_target="tpu_custom_call" | custom-call | tf_op jit(solution)/shard_map/finish/pallas_call | solution.py:516
Async XLA Ops:
  5.7 23.3 %all-to-all-start = ((f32[32,8,128]{2,1,0:T(8,128)}), f32[32,8,128]{2,1,0:T(8,128)}, u32[]{:S(2)}, u32[]{:S(2)}) async-start(f32[32,8,128]{2,1,0:T(8,128)} %get-tuple-element.29), calls=%async_computation | async-start | bytes 262144 | tf_op jit(solution)/shard_map/all_to_all | solution.py:592
  11.9 14.9 %collective-permute-start.2 = (f32[6,72,128]{2,1,0:T(8,128)S(1)}, f32[6,72,128]{2,1,0:T(8,128)S(1)}, u32[]{:S(2)}, u32[]{:S(2)}) collective-permute-start(f32[6,72,128]{2,1,0:T(8,128)S(1)} %get-tuple-element.26), channel_id=1, source_target_pairs={{0,8},{8,0},{16,24},{24,16},{1,9},{9,1},{17,25},{25,17},{2,10},{10... | collective-permute-start | bytes 663560 | tf_op jit(solution)/shard_map/ppermute | solution.py:596
  12.2 14.6 %collective-permute-start.3 = (f32[6,72,128]{2,1,0:T(8,128)S(1)}, f32[6,72,128]{2,1,0:T(8,128)S(1)}, u32[]{:S(2)}, u32[]{:S(2)}) collective-permute-start(f32[6,72,128]{2,1,0:T(8,128)S(1)} %get-tuple-element.27), channel_id=1, source_target_pairs={{8,16},{16,8},{9,17},{17,9},{10,18},{18,10},{11,19},{19,11},{12,20... | collective-permute-start | bytes 663560 | tf_op jit(solution)/shard_map/ppermute | solution.py:597
  16.2 2.8 %collective-permute-start = (f32[2,72,128]{2,1,0:T(8,128)S(1)}, f32[2,72,128]{2,1,0:T(8,128)S(1)}, u32[]{:S(2)}, u32[]{:S(2)}) collective-permute-start(f32[2,72,128]{2,1,0:T(8,128)S(1)} %get-tuple-element.23), channel_id=1, source_target_pairs={{0,1},{1,0},{2,3},{3,2},{4,5},{5,4},{6,7},{7,6},{8,9},{9,8},{10,11... | collective-permute-start | bytes 221192 | tf_op jit(solution)/shard_map/ppermute | solution.py:598
  17.2 5.6 %collective-permute-start.1 = (f32[2,72,128]{2,1,0:T(8,128)S(1)}, f32[2,72,128]{2,1,0:T(8,128)S(1)}, u32[]{:S(2)}, u32[]{:S(2)}) collective-permute-start(f32[2,72,128]{2,1,0:T(8,128)S(1)} %get-tuple-element.24), channel_id=1, source_target_pairs={{0,7},{1,2},{2,1},{3,4},{4,3},{5,6},{6,5},{7,0},{8,15},{9,10},{10,... | collective-permute-start | bytes 221192 | tf_op jit(solution)/shard_map/ppermute | solution.py:599

commit v3 on v2

v3 whole, which is shorter than its diff:
```python
import functools

import jax
import jax.numpy as jnp
import numpy as np
from jax import lax
from jax.experimental import pallas as pl
from jax.experimental.pallas import tpu as pltpu
from jax.sharding import PartitionSpec as P


LATERAL_ZONES = 16
CFL_NUMBER = 0.12
GAS_SCALE = 0.01
BETA = 0.7862
LANES = 128
EXTRA = 8
F32 = jnp.float32
VMEM = pltpu.MemorySpace.VMEM


def row_ids():
    return lax.broadcasted_iota(jnp.int32, (EXTRA, LANES), 0)


def split(value):
    high = value.astype(jnp.bfloat16)
    low = (value - high.astype(F32)).astype(jnp.bfloat16)
    return high, low


def fold_rows(value, op):
    parts = [value[8 * i : 8 * i + 8] for i in range(value.shape[0] // 8)]
    while len(parts) > 1:
        half = [op(parts[i], parts[i + 1]) for i in range(0, len(parts) - 1, 2)]
        parts = half + ([parts[-1]] if len(parts) % 2 else [])
    return parts[0]


def column_sum(value):
    return jnp.sum(fold_rows(value, jnp.add), axis=0, keepdims=True)


def write_matrix(mass_ref, size_ref, energy_ref, poly_ref, base_ref, slope_ref, crit_ref, mat_ref):
    species = mass_ref.shape[1]
    terms = poly_ref.shape[0] // species
    inverse = 1.0 / mass_ref[...]
    rows = lax.broadcasted_iota(jnp.int32, (species, species), 0)
    cols = lax.broadcasted_iota(jnp.int32, (species, species), 1)
    same = rows == cols
    column = jnp.sum(
        jnp.where(same, jnp.broadcast_to(inverse, (species, species)), 0.0), axis=1, keepdims=True
    )

    def put(start, block):
        high, low = split(block)
        high, low = high.astype(F32), low.astype(F32)
        mat_ref[start : start + block.shape[0], :] = jnp.concatenate(
            [high, low], axis=1
        ).astype(jnp.bfloat16)

    for k in range(terms):
        block = jnp.where(same, 0.0, poly_ref[k * species : (k + 1) * species, :])
        put(k * species, block * inverse)
    put(terms * species, size_ref[...] * inverse * column)
    put((terms + 1) * species, energy_ref[...] * inverse * column)
    lin = lax.broadcasted_iota(jnp.int32, (16, species), 0)
    block = jnp.where(lin == 0, 1.0, 0.0)
    for k, row in enumerate(
        (inverse, base_ref[...] * inverse, slope_ref[...] * inverse, crit_ref[...] * inverse)
    ):
        block = jnp.where(lin == k + 1, row, block)
    put((terms + 2) * species, block)


def mix_products(units, group, read, mat_ref, lin_ref, resist_ref, extra=None):
    ids = row_ids()

    def step(j, carry):
        pieces = [read(j, i) for i in range(group)]
        mass = [p[0] for p in pieces]
        species = mass[0].shape[0]
        terms = mat_ref.shape[0] // species - 2
        wide = jnp.concatenate(mass, axis=1)
        high, low = split(wide)
        stacked = jnp.concatenate([high, high, low, low], axis=0)
        both = jnp.concatenate([mat_ref[...], mat_ref[...]], axis=1)
        product = jnp.dot(both, stacked, preferred_element_type=F32)
        for i, (m, temper) in enumerate(pieces):
            part = product[:, i * LANES : (i + 1) * LANES]
            u = j * group + i
            logt = jnp.log(temper)
            total = part[(terms - 1) * species : terms * species]
            for k in range(terms - 2, -1, -1):
                total = total * logt + part[k * species : (k + 1) * species]
            resist_ref[u, 0:species, :] = total
            size = column_sum(m * part[terms * species : (terms + 1) * species])
            energy = column_sum(m * part[(terms + 1) * species : (terms + 2) * species])
            lin = part[(terms + 2) * species : (terms + 2) * species + 8]
            lin = jnp.where(ids == 5, size, jnp.where(ids == 6, energy, lin))
            lin = jnp.where(ids == 7, temper, lin)
            lin_ref[pl.ds(pl.multiple_of(u * 8, 8), 8), :] = lin
            if extra is not None:
                extra(j, i, u, temper, part[(terms + 2) * species : (terms + 2) * species + 1])
        return carry

    lax.fori_loop(0, units // group, step, 0)


def mix_cells(units, lin_ref, plane_ref):
    def plane(k):
        return lin_ref[pl.ds(k, units, stride=8), :]

    density, moles, base, slope, crit, size, energy, temper = [plane(k) for k in range(8)]
    reduced = temper * size / energy
    collision = (
        1.16145 * jnp.exp(-0.14874 * jnp.log(reduced))
        + 0.52487 * jnp.exp(-0.7732 * reduced)
        + 2.16178 * jnp.exp(-2.43787 * reduced)
    )
    inv_moles = 1.0 / moles
    mean_mass = density * inv_moles
    size_mix = size * inv_moles * inv_moles
    viscosity = (
        (40.785 * (0.809 * 0.809))
        * jnp.sqrt(mean_mass * temper)
        / (jnp.exp((2.0 / 3.0) * jnp.log(size_mix)) * collision)
    )
    heat_total = base + slope * temper
    excess = heat_total * inv_moles - 2.5
    ratio = reduced * (1.0 / 1.2593)
    zeta = 2.0 + 10.5 * ratio * ratio
    psi = 1.0 + excess * (0.215 + 0.28288 * excess - 1.061 * BETA + 0.26665 * zeta) / (
        0.6366 + BETA * zeta + (1.061 * BETA) * excess
    )
    conduct = 7.452 * viscosity * psi / mean_mass
    over = GAS_SCALE * temper * moles * moles / crit
    takahashi = 1.0 / (1.0 + 0.25 * over * over)
    front = density * takahashi * jnp.sqrt(temper) * (1.0 / GAS_SCALE)
    inv_density = 1.0 / density
    inv_heat = 1.0 / heat_total
    plane_ref[0] = front
    plane_ref[1] = inv_density
    plane_ref[2] = viscosity
    plane_ref[3] = conduct
    plane_ref[4] = inv_heat
    return jnp.maximum(viscosity * inv_density, conduct * inv_heat)


def coefficient_rows(plane_ref, u):
    ids = row_ids()
    visc = plane_ref[2, pl.ds(u, 1), :]
    cond = plane_ref[3, pl.ds(u, 1), :]
    return jnp.where(ids == 0, cond, jnp.where(ids < 4, visc, 0.0))


def mix_halo(units, group, state_ref, mat_ref, lin_ref, plane_ref, carried_ref):
    species = state_ref.shape[1] - EXTRA

    def read(j, i):
        u = j * group + i
        density = state_ref[u, species + 4 : species + 5, :]
        return state_ref[u, 0:species, :] * density, state_ref[u, species : species + 1, :]

    mix_products(units, group, read, mat_ref, lin_ref, carried_ref)
    mix_cells(units, lin_ref, plane_ref)

    def step(u, carry):
        front = plane_ref[0, pl.ds(u, 1), :]
        fraction = state_ref[u, 0:species, :]
        carried_ref[u, 0:species, :] = front * ((1.0 - fraction) / carried_ref[u, 0:species, :])
        carried_ref[u, species : species + EXTRA, :] = coefficient_rows(plane_ref, u)
        return carry

    lax.fori_loop(0, units, step, 0)


def pack_cells(ref, unit, tiles, start, per):
    reach = LANES // per
    rows = ref.shape[1]
    lanes = lax.broadcasted_iota(jnp.int32, (rows, LANES), 1)
    out = None
    for k in range(per):
        piece = ref[unit + k * tiles]
        turn = (k * reach - start) % LANES
        if turn:
            piece = pltpu.roll(piece, turn, 1)
        out = piece if k == 0 else jnp.where(lanes >= k * reach, piece, out)
    return out


def cell_copies(conc_hbm, temper_hbm, motion_hbm, base_ref, sem):
    copies = []
    for t in range(base_ref.shape[0]):
        start = 0
        for k, src in enumerate((conc_hbm, temper_hbm, motion_hbm)):
            dst = base_ref.at[t, pl.ds(start, src.shape[0])]
            part = src.at[:, pl.ds(t * LANES, LANES)]
            copies.append(pltpu.make_async_copy(part, dst, sem.at[3 * t + k]))
            start += src.shape[0]
    return copies


def mixture_kernel(
    conc_hbm, temper_hbm, motion_hbm, mass_hbm, size_hbm, energy_hbm, poly_hbm, base_hbm,
    slope_hbm, crit_hbm,
    state_ref, carried_ref, mat_ref, first_x, second_x, first_y, second_y, rate_ref,
    base_ref, mass_ref, size_ref, energy_ref, poly_ref, heat_ref, slope_ref, crit_ref, lin_ref, plane_ref,
    table_sem, cell_sem,
):
    tiles = base_ref.shape[0]
    width = temper_hbm.shape[0]
    species = mass_ref.shape[1]
    units = tiles * width
    cells = species * width
    pairs = (
        (mass_hbm, mass_ref), (size_hbm, size_ref), (energy_hbm, energy_ref),
        (poly_hbm, poly_ref), (base_hbm, heat_ref), (slope_hbm, slope_ref), (crit_hbm, crit_ref),
    )
    tables = [
        pltpu.make_async_copy(src, dst, table_sem.at[k]) for k, (src, dst) in enumerate(pairs)
    ]
    copies = cell_copies(conc_hbm, temper_hbm, motion_hbm, base_ref, cell_sem)
    for c in tables + copies:
        c.start()
    for c in tables:
        c.wait()
    write_matrix(
        mass_ref, size_ref, energy_ref, poly_ref, heat_ref, slope_ref, crit_ref, mat_ref
    )
    for c in copies:
        c.wait()
    ids = row_ids()

    batch = 2 if width % 2 == 0 else 1

    def place(j, i):
        return j * batch + i // tiles, i % tiles

    def read(j, i):
        x, t = place(j, i)
        mass = base_ref[t, pl.ds(x, species, stride=width), :]
        return mass, base_ref[t, pl.ds(cells + x, 1), :]

    def extra(j, i, u, temper, density):
        x, t = place(j, i)
        block = jnp.where(ids == 0, temper, jnp.where(ids == 4, density, 0.0))
        for c in range(3):
            row = base_ref[t, pl.ds(cells + (c + 1) * width + x, 1), :]
            block = jnp.where(ids == c + 1, row, block)
        state_ref[u, species : species + EXTRA, :] = block

    mix_products(units, batch * tiles, read, mat_ref, lin_ref, carried_ref, extra)
    rates = mix_cells(units, lin_ref, plane_ref)

    def step(x, best):
        for t in range(tiles):
            u = x * tiles + t
            front = plane_ref[0, pl.ds(u, 1), :]
            inv_density = plane_ref[1, pl.ds(u, 1), :]
            fraction = base_ref[t, pl.ds(x, species, stride=width), :] * inv_density
            share = (1.0 - fraction) / carried_ref[u, 0:species, :]
            state_ref[u, 0:species, :] = fraction
            carried_ref[u, 0:species, :] = front * share
            carried_ref[u, species : species + EXTRA, :] = coefficient_rows(plane_ref, u)
            state_ref[u, species + 5 : species + 6, :] = plane_ref[4, pl.ds(u, 1), :]
            state_ref[u, species + 6 : species + 7, :] = inv_density
            best = jnp.maximum(best, fold_rows(share, jnp.maximum) * (front * inv_density))
        return best

    best = lax.fori_loop(0, width, step, jnp.zeros((8, LANES), F32))
    top = jnp.maximum(jnp.max(best), jnp.max(rates))
    rate_ref[...] = jnp.full(rate_ref.shape, top, F32)

    even_x = lax.rem(lax.axis_index("gx"), 2) == 0
    upper = (width - 2) * tiles
    start_a = jnp.where(even_x, upper, 0)
    start_b = upper - start_a
    for k in range(2 * tiles):
        first_x[k] = state_ref[start_a + k]
        second_x[k] = state_ref[start_b + k]
    even_y = lax.rem(lax.axis_index("gy"), 2) == 0
    reach = 2 * LATERAL_ZONES
    per = LANES // reach
    for g in range(width // per):
        low = pack_cells(state_ref, g * per * tiles, tiles, 0, per)
        high = pack_cells(state_ref, g * per * tiles + tiles - 1, tiles, LANES - reach, per)
        first_y[g] = jnp.where(even_y, high, low)
        second_y[g] = jnp.where(even_y, low, high)


def weigh(before, here, after, beyond):
    value = 9.0 * (here + after) - (before + beyond)
    slope = 27.0 * (after - here) - (beyond - before)
    return value, slope


def only_value(before, here, after, beyond):
    return 9.0 * (here + after) - (before + beyond)


def z_shift(part, amount):
    zc = LATERAL_ZONES
    z_index = lax.broadcasted_iota(jnp.int32, part.shape, 1) % zc
    near = pltpu.roll(part, (LANES - amount) % LANES, 1)
    far = pltpu.roll(part, (zc - amount) if amount > 0 else LANES - (zc + amount), 1)
    if amount > 0:
        return jnp.where(z_index < zc - amount, near, far)
    return jnp.where(z_index >= -amount, near, far)


def face_weights(offset):
    value = np.select([offset == -1, offset == 0, offset == 1, offset == 2], [-1, 9, 9, -1], 0)
    slope = np.select([offset == -1, offset == 0, offset == 1, offset == 2], [1, -27, 27, -1], 0)
    return value, slope


def stencil_weights():
    zc = LATERAL_ZONES
    src, dst = np.meshgrid(np.arange(LANES), np.arange(LANES), indexing="ij")
    near = (src // zc) == (dst // zc)
    z_value, z_slope = face_weights(np.where(near, (src % zc - dst % zc + 1) % zc - 1, 9))

    def along_y(place):
        gap = place - dst
        return face_weights(np.where(gap % zc == 0, gap // zc, 9))

    y_value, y_slope = along_y(src)
    lent = along_y(np.where(src < 2 * zc, src + LANES, src - LANES))
    blocks = np.concatenate([z_value, y_value, z_slope, y_slope, *lent], axis=1)
    return np.concatenate([blocks, blocks], axis=0).astype(jnp.bfloat16)


def face_flux(f, h, species):
    value, slope = weigh(*f)
    product = only_value(*h) * slope
    drift = column_sum(product[:species]) * 0.0625
    return jnp.concatenate(
        [product[:species] - value[:species] * drift, product[species:]], axis=0
    )


def drifted(product, value, species):
    drift = column_sum(product[:species]) * 0.0625
    return jnp.concatenate([product[:species] - value[:species] * drift, product[species:]], axis=0)


def inner_kernel(
    batch, tiles, state_ref, carried_ref, weight_hbm, mat_ref, rate_ref, mat_out, weight_ref, sem
):
    units, rows, _ = state_ref.shape
    species = rows - EXTRA
    width = units // tiles
    zc = LATERAL_ZONES
    reach = 2 * zc
    wide = lax.broadcasted_iota(jnp.int32, (rows, LANES), 1)
    copy = pltpu.make_async_copy(weight_hbm, weight_ref, sem)
    copy.start()
    mat_out[...] = mat_ref[...]

    def along(t, carry):
        before = None
        for face in range(2, width - 1):
            f = [state_ref[(face + k) * tiles + t] for k in (-2, -1, 0, 1)]
            h = [carried_ref[(face + k) * tiles + t] for k in (-2, -1, 0, 1)]
            flux = face_flux(f, h, species)
            u = (face - 1) * tiles + t
            rate_ref[u] = flux if before is None else flux - before
            before = flux
        u = (width - 2) * tiles + t
        rate_ref[u] = -before
        for x in (0, width - 1):
            rate_ref[x * tiles + t] = jnp.zeros((rows, LANES), F32)
        return carry

    lax.fori_loop(0, tiles, along, 0)
    copy.wait()

    def wings(ref, j):
        own, lent = [], []
        for b in range(batch):
            f = [ref[(j * batch + b) * tiles + t] for t in range(tiles)]
            own += f
            for t in range(tiles):
                lent.append(jnp.where(wide < reach, f[(t + 1) % tiles], f[t - 1]))
        return [jnp.concatenate(split(jnp.concatenate(p, axis=0)), axis=1) for p in (own, lent)]

    def dot(a, start, stop):
        return jnp.dot(a, weight_ref[:, start * LANES : stop * LANES], preferred_element_type=F32)

    def work(j, carry):
        own, lent = wings(state_ref, j)
        first = dot(own, 0, 4)
        second = dot(lent, 4, 6)
        own, lent = wings(carried_ref, j)
        third = dot(own, 0, 2)
        fourth = dot(lent, 4, 5)
        for b in range(batch):
            fluxes = []
            for t in range(tiles):
                u = (j * batch + b) * tiles + t
                i = b * tiles + t
                rs = slice(i * rows, (i + 1) * rows)
                part = lambda m, k: m[rs, k * LANES : (k + 1) * LANES]
                flux = drifted(part(third, 0) * part(first, 2), part(first, 0), species)
                rate_ref[u] = rate_ref[u] + (flux - z_shift(flux, -1))
                value = part(first, 1) + part(second, 0)
                slope = part(first, 3) + part(second, 1)
                flux = drifted((part(third, 1) + part(fourth, 0)) * slope, value, species)
                if t == 0:
                    flux = jnp.where(wide >= zc, flux, 0.0)
                if t == tiles - 1:
                    flux = jnp.where(wide < LANES - reach, flux, 0.0)
                fluxes.append(flux)
            turned = [pltpu.roll(flux, zc, 1) for flux in fluxes]
            for t in range(tiles):
                u = (j * batch + b) * tiles + t
                back = jnp.where(wide >= zc, turned[t], turned[t - 1] if t > 0 else 0.0)
                rate_ref[u] = rate_ref[u] + (fluxes[t] - back)
        return carry

    lax.fori_loop(0, width // batch, work, 0)


def rim_kernel(
    state_ref, carried_ref, mat_ref, first_y, second_y, first_x, second_x, partial_ref,
    rate_ref,
    halo_ref, halo_carried, lin_ref, plane_ref, edge_ref, pack_ref, halo_sem,
):
    units, rows, _ = state_ref.shape
    species = rows - EXTRA
    packs = first_y.shape[0]
    half = first_x.shape[0]
    tiles = half // 2
    width = units // tiles
    zc = LATERAL_ZONES
    reach = 2 * zc
    per = LANES // reach
    me, peers = lax.axis_index("gx"), lax.axis_size("gx")
    even_x = lax.rem(me, 2) == 0
    even_y = lax.rem(lax.axis_index("gy"), 2) == 0
    at_start, at_end = me == 0, me == peers - 1
    skip = 2 * packs
    low_x, low_y = jnp.where(even_x, half, 0), jnp.where(even_y, packs, 0)
    halos = [
        pltpu.make_async_copy(src, halo_ref.at[pl.ds(start, src.shape[0])], halo_sem.at[k])
        for k, (src, start) in enumerate(
            (
                (first_y, low_y),
                (second_y, packs - low_y),
                (first_x, skip + low_x),
                (second_x, skip + half - low_x),
            )
        )
    ]
    for c in halos:
        c.start()
    for g in range(packs):
        unit = g * per * tiles
        last = unit + tiles - 1
        for k, ref in enumerate((state_ref, carried_ref)):
            for i, (at, start) in enumerate(
                ((unit, 0), (unit, reach), (last, LANES - 2 * reach), (last, LANES - reach))
            ):
                pack_ref[(4 * k + i) * packs + g] = pack_cells(ref, at, tiles, start, per)

    for c in halos:
        c.wait()

    @pl.when(at_start)
    def _():
        for k in range(half):
            halo_ref[skip + k] = state_ref[k % tiles]

    @pl.when(at_end)
    def _():
        for k in range(half):
            halo_ref[skip + half + k] = state_ref[units - tiles + k % tiles]

    total = skip + 2 * half
    group = next(n for n in (8, 6, 4, 3, 2, 1) if total % n == 0)
    mix_halo(total, group, halo_ref, mat_ref, lin_ref, plane_ref, halo_carried)

    ids = row_ids()
    wide = lax.broadcasted_iota(jnp.int32, (rows, LANES), 1)
    lower = wide % reach < zc

    def between(p, q):
        return jnp.where(lower, pltpu.roll(p, LANES - zc, 1), pltpu.roll(q, zc, 1))

    for g in range(packs):
        stencils = []
        for i, halo in enumerate((halo_ref, halo_carried)):
            below, above = halo[g], halo[packs + g]
            low, up, down, high = [pack_ref[(4 * i + k) * packs + g] for k in range(4)]
            stencils.append(
                (
                    (below, between(below, low), low, between(low, up)),
                    (between(down, high), high, between(high, above), above),
                )
            )
        flux = face_flux(stencils[0][0], stencils[1][0], species)
        edge_ref[g] = jnp.where(lower, pltpu.roll(flux, LANES - zc, 1), 0.0) - flux
        flux = face_flux(stencils[0][1], stencils[1][1], species)
        edge_ref[packs + g] = flux - jnp.where(lower, 0.0, pltpu.roll(flux, zc, 1))

    for t in range(tiles):

        def row(inner, outer, x):
            if x < 0:
                return outer[skip + (x + 2) * tiles + t]
            if x >= width:
                return outer[skip + half + (x - width) * tiles + t]
            return inner[x * tiles + t]

        flux = {}
        for face in (0, 1, width - 1, width):
            f = [row(state_ref, halo_ref, face + k) for k in (-2, -1, 0, 1)]
            h = [row(carried_ref, halo_carried, face + k) for k in (-2, -1, 0, 1)]
            flux[face] = face_flux(f, h, species)
        for x in range(width):
            u = x * tiles + t
            g, k = divmod(x, per)
            total = partial_ref[u]
            if x + 1 in flux:
                total = total + flux[x + 1]
            if x in flux:
                total = total - flux[x]
            if t == 0:
                edge = edge_ref[g]
                edge = pltpu.roll(edge, LANES - k * reach, 1) if k else edge
                total = total + jnp.where(wide < reach, edge, 0.0)
            if t == tiles - 1:
                edge = edge_ref[packs + g]
                turn = (LANES - (k + 1) * reach) % LANES
                edge = pltpu.roll(edge, turn, 1) if turn else edge
                total = total + jnp.where(wide >= LANES - reach, edge, 0.0)
            inv_heat = state_ref[u, species + 5 : species + 6, :]
            inv_density = state_ref[u, species + 6 : species + 7, :]
            scale = jnp.where(ids == 0, inv_heat, inv_density)
            total = jnp.concatenate([total[:species], total[species:] * scale], axis=0)
            rate_ref[u] = total


def finish_kernel(
    state_ref, rate_ref, top_ref,
    conc_next, temper_next, motion_next, interval_next,
    next_ref, interval_ref, sem,
):
    tiles, _, _ = next_ref.shape
    units, rows, _ = state_ref.shape
    species = rows - EXTRA
    width = units // tiles
    interval = CFL_NUMBER / jnp.max(top_ref[...], axis=(0, 1), keepdims=True)
    interval_ref[...] = interval
    factor = interval * (1.0 / 384.0)
    outs = [pltpu.make_async_copy(interval_ref, interval_next, sem.at[3 * tiles])]
    outs[0].start()
    for t in range(tiles):
        for x in range(width):
            u = x * tiles + t
            density = state_ref[u, species + 4 : species + 5, :]
            here = jnp.concatenate(
                [state_ref[u, 0:species, :] * density, state_ref[u, species:, :]], axis=0
            )
            next_ref[t, pl.ds(x, rows, stride=width), :] = here + factor * rate_ref[u]
        start = 0
        for k, dst in enumerate((conc_next, temper_next, motion_next)):
            src = next_ref.at[t, pl.ds(start, dst.shape[0])]
            part = dst.at[:, pl.ds(t * LANES, LANES)]
            outs.append(pltpu.make_async_copy(src, part, sem.at[3 * t + k]))
            outs[-1].start()
            start += dst.shape[0]
    for c in outs:
        c.wait()


def call(kernel, outs, ins, scratch=()):
    shapes, specs = [], []
    for shape, dtype, place in outs:
        space = {True: pltpu.VMEM, pl.ANY: pltpu.HBM}.get(place, jax.ShapeDtypeStruct)
        shapes.append(space(shape, dtype))
        specs.append(pl.BlockSpec(memory_space=pl.ANY if place is pl.ANY else VMEM))
    run = pl.pallas_call(
        kernel,
        out_shape=shapes,
        in_specs=[
            pl.BlockSpec(memory_space={True: VMEM, pl.ANY: pltpu.HBM, None: pl.ANY}[m]) for m in ins
        ],
        out_specs=specs,
        scratch_shapes=list(scratch),
        compiler_params=pltpu.CompilerParams(vmem_limit_bytes=16 << 20),
    )

    def apply(*args):
        return run(
            *[
                a
                if m is None
                else pltpu.with_memory_space_constraint(a, pltpu.VMEM if m is True else pltpu.HBM)
                for a, m in zip(args, ins)
            ]
        )

    return apply


def body(
    component_concentration,
    thermal_level,
    motion_vector,
    component_weight_per_mole,
    collision_size_third,
    potential_depth_volume,
    binary_drag_logpoly,
    specific_warmth_intercept,
    specific_warmth_gradient,
    component_threshold_stress,
):
    species, width, line = component_concentration.shape
    terms = binary_drag_logpoly.shape[0]
    tiles = line // LANES
    units = width * tiles
    rows = species + EXTRA
    per = LANES // (2 * LATERAL_ZONES)
    packs = width // per
    nx, ny = lax.axis_size("gx"), lax.axis_size("gy")
    devices = nx * ny
    conc = component_concentration.reshape(species * width, line)
    motion = motion_vector.reshape(3 * width, line)
    mat_rows = (terms + 2) * species + 16
    count = (species + 4) * width
    keep = True
    field = ((units, rows, LANES), F32, keep)
    mix_scratch = lambda n: [pltpu.VMEM((n * 8, LANES), F32), pltpu.VMEM((5, n, LANES), F32)]
    state, carried, mat, first_x, second_x, first_y, second_y, rate = call(
        mixture_kernel,
        [
            field,
            field,
            ((mat_rows, 2 * species), jnp.bfloat16, keep),
            ((2 * tiles, rows, LANES), F32, keep),
            ((2 * tiles, rows, LANES), F32, keep),
            ((packs, rows, LANES), F32, keep),
            ((packs, rows, LANES), F32, keep),
            ((devices, LANES), F32, keep),
        ],
        [pl.ANY] * 10,
        [
            pltpu.VMEM((tiles, count, LANES), F32),
            pltpu.VMEM((1, species), F32),
            pltpu.VMEM((species, species), F32),
            pltpu.VMEM((species, species), F32),
            pltpu.VMEM((terms * species, species), F32),
            pltpu.VMEM((1, species), F32),
            pltpu.VMEM((1, species), F32),
            pltpu.VMEM((1, species), F32),
        ]
        + mix_scratch(units)
        + [pltpu.SemaphoreType.DMA((n,)) for n in (7, 3 * tiles)],
    )(
        conc,
        thermal_level,
        motion,
        component_weight_per_mole[None],
        collision_size_third,
        potential_depth_volume,
        binary_drag_logpoly.reshape(terms * species, species),
        specific_warmth_intercept[None],
        specific_warmth_gradient[None],
        component_threshold_stress[None],
    )
    top = lax.all_to_all(rate, ("gx", "gy"), 0, 0, tiled=True)
    pair_first = lambda n: [(i, i ^ 1) for i in range(n)]
    pair_second = lambda n: [(i, (i + 1) % n if i % 2 else (i - 1) % n) for i in range(n)]
    inside = [(i, j) for i, j in pair_second(nx) if abs(i - j) == 1]
    got_first_x = lax.ppermute(first_x, "gx", pair_first(nx))
    got_second_x = lax.ppermute(second_x, "gx", inside)
    got_first_y = lax.ppermute(first_y, "gy", pair_first(ny))
    got_second_y = lax.ppermute(second_y, "gy", pair_second(ny))
    batch = 2 if width % 2 == 0 else 1
    weights = jnp.asarray(stencil_weights())
    inner, mat = call(
        functools.partial(inner_kernel, batch, tiles),
        [
            field,
            ((mat_rows, 2 * species), jnp.bfloat16, keep),
        ],
        [keep, keep, pl.ANY, keep],
        [pltpu.VMEM(weights.shape, weights.dtype), pltpu.SemaphoreType.DMA(())],
    )(state, carried, weights, mat)
    halos = 2 * packs + 4 * tiles
    (total,) = call(
        rim_kernel,
        [field],
        [keep] * 3 + [None] * 4 + [keep],
        [
            pltpu.VMEM((halos, rows, LANES), F32),
            pltpu.VMEM((halos, rows, LANES), F32),
        ]
        + mix_scratch(halos)
        + [
            pltpu.VMEM((2 * packs, rows, LANES), F32),
            pltpu.VMEM((8 * packs, rows, LANES), F32),
            pltpu.SemaphoreType.DMA((4,)),
        ],
    )(
        state,
        carried,
        mat,
        got_first_y,
        got_second_y,
        got_first_x,
        got_second_x,
        inner,
    )
    conc_next, temper_next, motion_next, interval = call(
        finish_kernel,
        [
            (conc.shape, F32, pl.ANY),
            (thermal_level.shape, F32, pl.ANY),
            (motion.shape, F32, pl.ANY),
            ((1, 1), F32, pl.ANY),
        ],
        [keep] * 3,
        [
            pltpu.VMEM((tiles, rows * width, LANES), F32),
            pltpu.VMEM((1, 1), F32),
            pltpu.SemaphoreType.DMA((3 * tiles + 1,)),
        ],
    )(state, total, top)
    return (
        conc_next.reshape(component_concentration.shape),
        motion_next.reshape(motion_vector.shape),
        temper_next,
        interval.reshape(()),
    )


def solution(mesh):
    in_specs = (
        P(None, "gx", "gy"),
        P("gx", "gy"),
        P(None, "gx", "gy"),
    ) + (P(),) * 7
    out_specs = (P(None, "gx", "gy"), P(None, "gx", "gy"), P("gx", "gy"), P())
    return jax.shard_map(body, mesh=mesh, in_specs=in_specs, out_specs=out_specs, check_vma=False)
```

time: 31.8 us -> 25.3 us (0.80)
  the two profiles are of different devices: /device:TPU:27 before, /device:TPU:0 now
where the time goes in v3:
time: 25.3 us; the launch traced here: 25.1 us
  starting transfers between devices  12.1 us (48%)
  Pallas kernels  12 us (47%)
  between operations  0.72 us (3%)
  waiting for transfers between devices  0.27 us (1%)
    pallas_call x4, Pallas kernels, apply(): run(*[a if m is None else pltpu.with_memory_space_constraint(a, pltpu.VME...  12 us
    all_to_all x1, starting transfers between devices, body(): top = lax.all_to_all(rate, ('gx', 'gy'), 0, 0, tiled=True)  4.58 us
    ppermute x1, starting transfers between devices, body(): got_second_y = lax.ppermute(second_y, 'gy', pair_second(ny))  3.7 us
    ppermute x1, starting transfers between devices, body(): got_first_x = lax.ppermute(first_x, 'gx', pair_first(nx))  3.03 us
    ppermute x1, starting transfers between devices, body(): got_second_x = lax.ppermute(second_x, 'gx', inside)  0.66 us
  transfers between devices with their start and end apart: 5, of which 1 were waited for; matrix products, arithmetic and copies ran while one was open for 0% of the time, Pallas kernels for 27%

profile of v3, /device:TPU:0, one launch (start us, length us, event | category | flops | bytes accessed | tf_op | source)
XLA Modules:
  0.0 25.1 jit_solution(3190291439131975565)
XLA Ops:
  0.6 4.1 %shard_map.138 = (f32[24,72,128]{2,1,0:T(8,128)S(1)}, f32[24,72,128]{2,1,0:T(8,128)S(1)}, bf16[400,128]{1,0:T(8,128)(2,1)S(1)}, f32[6,72,128]{2,1,0:T(8,128)S(1)...) custom-call(f32[512,384]{1,0:T(8,128)} %bitcast.15, ...), custom_call_target="tpu_custom_call" | custom-call | tf_op jit(solution)/shard_map/pallas_call | solution.py:596
  4.7 3.0 %collective-permute-start.2 = (f32[6,72,128]{2,1,0:T(8,128)S(1)}, f32[6,72,128]{2,1,0:T(8,128)S(1)}, u32[]{:S(2)}, u32[]{:S(2)}) collective-permute-start(f32[6,72,128]{2,1,0:T(8,128)S(1)} %get-tuple-element.24), channel_id=1, source_target_pairs={{0,8},{8,0},{16,24},{24,16},{1,9},{9,1},{17,25},{25,17},{2,10},{10... | collective-permute-start | bytes 663560 | tf_op jit(solution)/shard_map/ppermute | solution.py:677
  7.7 0.7 %collective-permute-start.3 = (f32[6,72,128]{2,1,0:T(8,128)S(1)}, f32[6,72,128]{2,1,0:T(8,128)S(1)}, u32[]{:S(2)}, u32[]{:S(2)}) collective-permute-start(f32[6,72,128]{2,1,0:T(8,128)S(1)} %get-tuple-element.25), channel_id=1, source_target_pairs={{8,16},{16,8},{9,17},{17,9},{10,18},{18,10},{11,19},{19,11},{12,20... | collective-permute-start | bytes 663560 | tf_op jit(solution)/shard_map/ppermute | solution.py:678
  8.4 0.1 collective-permute-start
  8.5 3.7 %collective-permute-start.1 = (f32[2,72,128]{2,1,0:T(8,128)S(1)}, f32[2,72,128]{2,1,0:T(8,128)S(1)}, u32[]{:S(2)}, u32[]{:S(2)}) collective-permute-start(f32[2,72,128]{2,1,0:T(8,128)S(1)} %get-tuple-element.23), channel_id=1, source_target_pairs={{0,7},{1,2},{2,1},{3,4},{4,3},{5,6},{6,5},{7,0},{8,15},{9,10},{10,... | collective-permute-start | bytes 221192 | tf_op jit(solution)/shard_map/ppermute | solution.py:680
  12.2 4.6 %all-to-all-start = ((f32[32,1,128]{2,1,0:T(1,128)}), f32[32,1,128]{2,1,0:T(1,128)S(1)}, u32[]{:S(2)}, u32[]{:S(2)}) async-start(f32[32,1,128]{2,1,0:T(1,128)} %bitcast.8), calls=%async_computation | async-start | bytes 32768 | tf_op jit(solution)/shard_map/all_to_all | solution.py:673
  16.8 3.5 %shard_map.139 = (f32[24,72,128]{2,1,0:T(8,128)S(1)}, bf16[400,128]{1,0:T(8,128)(2,1)S(1)}) custom-call(f32[24,72,128]{2,1,0:T(8,128)S(1)} %get-tuple-element.18.state_ref, f32[24,72,128]{2,1,0:T(8,128)S(1)} %get-tuple-element.19.carried_ref, bf16[256,768]{1,0:T(8,128)(2,1)} %constant.2.clone.weight_hbm, bf16[400,128]{1,0:T(8,128)(2,1)S(1)} %get-tuple-element.20.mat_ref), custom_call_target="tpu_custom_call" | custom-call | tf_op jit(solution)/shard_map/pallas_call | solution.py:596
  20.3 0.0 collective-permute-done.first_y
  20.3 0.0 collective-permute-done.1.second_y
  20.3 0.0 collective-permute-done.2.first_x
  20.3 0.0 collective-permute-done.3.second_x
  20.3 3.3 %shard_map.140.rate_ref = f32[24,72,128]{2,1,0:T(8,128)S(1)} custom-call(f32[24,72,128]{2,1,0:T(8,128)S(1)} %get-tuple-element.18.state_ref, f32[24,72,128]{2,1,0:T(8,128)S(1)} %get-tuple-element.19.carried_ref, bf16[400,128]{1,0:T(8,128)(2,1)S(1)} %get-tuple-element.21.mat_ref, f32[2,72,128]{2,1,0:T(8,128)S(1)} %collective-permute-done.first_y, ...), custom_call_target="tpu_custom_call" | custom-call | tf_op jit(solution)/shard_map/pallas_call | solution.py:596
  23.6 0.3 %all-to-all-done = f32[32,1,128]{2,1,0:T(1,128)S(1)} async-done(((f32[32,1,128]{2,1,0:T(1,128)}), f32[32,1,128]{2,1,0:T(1,128)S(1)}, u32[]{:S(2)}, u32[]{:S(2)}) %all-to-all-start) | async-done | bytes 16416 | tf_op jit(solution)/shard_map/all_to_all | solution.py:673
  23.9 1.2 %shard_map.141 = (f32[512,384]{1,0:T(8,128)}, f32[8,384]{1,0:T(8,128)}, f32[24,384]{1,0:T(8,128)}, f32[1,1]{1,0:T(1,128)}) custom-call(f32[24,72,128]{2,1,0:T(8,128)S(1)} %get-tuple-element.18.state_ref, f32[24,72,128]{2,1,0:T(8,128)S(1)} %shard_map.140.rate_ref, f32[32,128]{1,0:T(8,128)S(1)} %bitcast.14), custom_call_target="tpu_custom_call" | custom-call | tf_op jit(solution)/shard_map/pallas_call | solution.py:596
Async XLA Ops:
  4.7 15.6 %collective-permute-start.2 = (f32[6,72,128]{2,1,0:T(8,128)S(1)}, f32[6,72,128]{2,1,0:T(8,128)S(1)}, u32[]{:S(2)}, u32[]{:S(2)}) collective-permute-start(f32[6,72,128]{2,1,0:T(8,128)S(1)} %get-tuple-element.24), channel_id=1, source_target_pairs={{0,8},{8,0},{16,24},{24,16},{1,9},{9,1},{17,25},{25,17},{2,10},{10... | collective-permute-start | bytes 663560 | tf_op jit(solution)/shard_map/ppermute | solution.py:677
  7.7 12.6 %collective-permute-start.3 = (f32[6,72,128]{2,1,0:T(8,128)S(1)}, f32[6,72,128]{2,1,0:T(8,128)S(1)}, u32[]{:S(2)}, u32[]{:S(2)}) collective-permute-start(f32[6,72,128]{2,1,0:T(8,128)S(1)} %get-tuple-element.25), channel_id=1, source_target_pairs={{8,16},{16,8},{9,17},{17,9},{10,18},{18,10},{11,19},{19,11},{12,20... | collective-permute-start | bytes 663560 | tf_op jit(solution)/shard_map/ppermute | solution.py:678
  8.4 11.9 %collective-permute-start = (f32[2,72,128]{2,1,0:T(8,128)S(1)}, f32[2,72,128]{2,1,0:T(8,128)S(1)}, u32[]{:S(2)}, u32[]{:S(2)}) collective-permute-start(f32[2,72,128]{2,1,0:T(8,128)S(1)} %get-tuple-element.22), channel_id=1, source_target_pairs={{0,1},{1,0},{2,3},{3,2},{4,5},{5,4},{6,7},{7,6},{8,9},{9,8},{10,11... | collective-permute-start | bytes 221192 | tf_op jit(solution)/shard_map/ppermute | solution.py:679
  8.5 11.8 %collective-permute-start.1 = (f32[2,72,128]{2,1,0:T(8,128)S(1)}, f32[2,72,128]{2,1,0:T(8,128)S(1)}, u32[]{:S(2)}, u32[]{:S(2)}) collective-permute-start(f32[2,72,128]{2,1,0:T(8,128)S(1)} %get-tuple-element.23), channel_id=1, source_target_pairs={{0,7},{1,2},{2,1},{3,4},{4,3},{5,6},{6,5},{7,0},{8,15},{9,10},{10,... | collective-permute-start | bytes 221192 | tf_op jit(solution)/shard_map/ppermute | solution.py:680
  12.2 11.7 %all-to-all-start = ((f32[32,1,128]{2,1,0:T(1,128)}), f32[32,1,128]{2,1,0:T(1,128)S(1)}, u32[]{:S(2)}, u32[]{:S(2)}) async-start(f32[32,1,128]{2,1,0:T(1,128)} %bitcast.8), calls=%async_computation | async-start | bytes 32768 | tf_op jit(solution)/shard_map/all_to_all | solution.py:673

commit v4 on v3

--- a/solution.py
+++ b/solution.py
@@ -73,7 +73,7 @@
     put((terms + 2) * species, block)
 
 
-def mix_products(units, group, read, mat_ref, lin_ref, resist_ref, extra=None):
+def mix_products(units, group, read, mat_ref, lin_ref, resist_ref, extra=None, unit=None, ready=None):
     ids = row_ids()
 
     def step(j, carry):
@@ -88,7 +88,7 @@
         product = jnp.dot(both, stacked, preferred_element_type=F32)
         for i, (m, temper) in enumerate(pieces):
             part = product[:, i * LANES : (i + 1) * LANES]
-            u = j * group + i
+            u = j * group + i if unit is None else unit(j, i)
             logt = jnp.log(temper)
             total = part[(terms - 1) * species : terms * species]
             for k in range(terms - 2, -1, -1):
@@ -99,12 +99,18 @@
             lin = part[(terms + 2) * species : (terms + 2) * species + 8]
             lin = jnp.where(ids == 5, size, jnp.where(ids == 6, energy, lin))
             lin = jnp.where(ids == 7, temper, lin)
-            lin_ref[pl.ds(pl.multiple_of(u * 8, 8), 8), :] = lin
+            row = u * 8 if isinstance(u, int) else pl.multiple_of(u * 8, 8)
+            lin_ref[pl.ds(row, 8), :] = lin
             if extra is not None:
                 extra(j, i, u, temper, part[(terms + 2) * species : (terms + 2) * species + 1])
         return carry
 
-    lax.fori_loop(0, units // group, step, 0)
+    if ready is None:
+        lax.fori_loop(0, units // group, step, 0)
+    else:
+        for j in range(units // group):
+            ready(j)
+            step(j, 0)
 
 
 def mix_cells(units, lin_ref, plane_ref):
@@ -204,9 +210,9 @@
 def mixture_kernel(
     conc_hbm, temper_hbm, motion_hbm, mass_hbm, size_hbm, energy_hbm, poly_hbm, base_hbm,
     slope_hbm, crit_hbm,
-    state_ref, carried_ref, mat_ref, first_x, second_x, first_y, second_y, rate_ref,
-    base_ref, mass_ref, size_ref, energy_ref, poly_ref, heat_ref, slope_ref, crit_ref, lin_ref, plane_ref,
-    table_sem, cell_sem,
+    state_ref, carried_ref, mat_ref, first_x, second_x, first_y, second_y, rate_hbm,
+    rate_ref, base_ref, mass_ref, size_ref, energy_ref, poly_ref, heat_ref, slope_ref, crit_ref, lin_ref, plane_ref,
+    table_sem, cell_sem, rate_sem,
 ):
     tiles = base_ref.shape[0]
     width = temper_hbm.shape[0]
@@ -228,29 +234,25 @@
     write_matrix(
         mass_ref, size_ref, energy_ref, poly_ref, heat_ref, slope_ref, crit_ref, mat_ref
     )
-    for c in copies:
-        c.wait()
     ids = row_ids()
 
-    batch = 2 if width % 2 == 0 else 1
-
-    def place(j, i):
-        return j * batch + i // tiles, i % tiles
-
-    def read(j, i):
-        x, t = place(j, i)
+    def ready(t):
+        for c in copies if t == 0 else ():
+            c.wait()
+
+    def read(t, x):
         mass = base_ref[t, pl.ds(x, species, stride=width), :]
         return mass, base_ref[t, pl.ds(cells + x, 1), :]
 
-    def extra(j, i, u, temper, density):
-        x, t = place(j, i)
+    def extra(t, x, u, temper, density):
         block = jnp.where(ids == 0, temper, jnp.where(ids == 4, density, 0.0))
         for c in range(3):
             row = base_ref[t, pl.ds(cells + (c + 1) * width + x, 1), :]
             block = jnp.where(ids == c + 1, row, block)
         state_ref[u, species : species + EXTRA, :] = block
 
-    mix_products(units, batch * tiles, read, mat_ref, lin_ref, carried_ref, extra)
+    unit = lambda t, x: x * tiles + t
+    mix_products(units, width, read, mat_ref, lin_ref, carried_ref, extra, unit, ready)
     rates = mix_cells(units, lin_ref, plane_ref)
 
     def step(x, best):
@@ -268,9 +270,13 @@
             best = jnp.maximum(best, fold_rows(share, jnp.maximum) * (front * inv_density))
         return best
 
-    best = lax.fori_loop(0, width, step, jnp.zeros((8, LANES), F32))
+    best = jnp.zeros((8, LANES), F32)
+    for x in range(width):
+        best = step(x, best)
     top = jnp.maximum(jnp.max(best), jnp.max(rates))
     rate_ref[...] = jnp.full(rate_ref.shape, top, F32)
+    send = pltpu.make_async_copy(rate_ref, rate_hbm, rate_sem)
+    send.start()
 
     even_x = lax.rem(lax.axis_index("gx"), 2) == 0
     upper = (width - 2) * tiles
@@ -287,6 +293,7 @@
         high = pack_cells(state_ref, g * per * tiles + tiles - 1, tiles, LANES - reach, per)
         first_y[g] = jnp.where(even_y, high, low)
         second_y[g] = jnp.where(even_y, low, high)
+    send.wait()
 
 
 def weigh(before, here, after, beyond):
@@ -643,10 +650,11 @@
             ((2 * tiles, rows, LANES), F32, keep),
             ((packs, rows, LANES), F32, keep),
             ((packs, rows, LANES), F32, keep),
-            ((devices, LANES), F32, keep),
+            ((devices, LANES), F32, pl.ANY),
         ],
         [pl.ANY] * 10,
         [
+            pltpu.VMEM((devices, LANES), F32),
             pltpu.VMEM((tiles, count, LANES), F32),
             pltpu.VMEM((1, species), F32),
             pltpu.VMEM((species, species), F32),
@@ -657,7 +665,8 @@
             pltpu.VMEM((1, species), F32),
         ]
         + mix_scratch(units)
-        + [pltpu.SemaphoreType.DMA((n,)) for n in (7, 3 * tiles)],
+        + [pltpu.SemaphoreType.DMA((7,)), pltpu.SemaphoreType.DMA((3 * tiles,))]
+        + [pltpu.SemaphoreType.DMA(())],
     )(
         conc,
         thermal_level,

time: 25.3 us -> 24.7 us (0.976)
  Pallas kernels: 12 us -> 11.4 us
    pallas_call x4, Pallas kernels: 12 us -> 11.4 us  [apply(): run(*[a if m is None else pltpu.with_memory_space_constraint(a, pltpu.VME...]
  transfers between devices with their start and end apart: 5 -> 5, of which waited for: 1 -> 1; matrix products, arithmetic and copies ran while one was open for 0% -> 0% of each run, Pallas kernels for 27% -> 28%
where the time goes in v4:
time: 24.7 us; the launch traced here: 24.5 us
  starting transfers between devices  12.1 us (49%)
  Pallas kernels  11.4 us (46%)
  between operations  0.72 us (3%)
  waiting for transfers between devices  0.27 us (1%)
    pallas_call x4, Pallas kernels, apply(): run(*[a if m is None else pltpu.with_memory_space_constraint(a, pltpu.VME...  11.4 us
    all_to_all x1, starting transfers between devices, body(): top = lax.all_to_all(rate, ('gx', 'gy'), 0, 0, tiled=True)  4.58 us
    ppermute x1, starting transfers between devices, body(): got_second_y = lax.ppermute(second_y, 'gy', pair_second(ny))  3.7 us
    ppermute x1, starting transfers between devices, body(): got_first_x = lax.ppermute(first_x, 'gx', pair_first(nx))  3.04 us
    ppermute x1, starting transfers between devices, body(): got_second_x = lax.ppermute(second_x, 'gx', inside)  0.66 us
  transfers between devices with their start and end apart: 5, of which 1 were waited for; matrix products, arithmetic and copies ran while one was open for 0% of the time, Pallas kernels for 28%

profile of v4, /device:TPU:0, one launch (start us, length us, event | category | flops | bytes accessed | tf_op | source)
XLA Modules:
  0.0 24.5 jit_solution(2175581097024174455)
XLA Ops:
  0.6 3.5 %shard_map.138 = (f32[24,72,128]{2,1,0:T(8,128)S(1)}, f32[24,72,128]{2,1,0:T(8,128)S(1)}, bf16[400,128]{1,0:T(8,128)(2,1)S(1)}, f32[6,72,128]{2,1,0:T(8,128)S(1)...) custom-call(f32[512,384]{1,0:T(8,128)} %bitcast.15, ...), custom_call_target="tpu_custom_call" | custom-call | tf_op jit(solution)/shard_map/pallas_call | solution.py:603
  4.1 3.0 %collective-permute-start.2 = (f32[6,72,128]{2,1,0:T(8,128)S(1)}, f32[6,72,128]{2,1,0:T(8,128)S(1)}, u32[]{:S(2)}, u32[]{:S(2)}) collective-permute-start(f32[6,72,128]{2,1,0:T(8,128)S(1)} %get-tuple-element.24), channel_id=1, source_target_pairs={{0,8},{8,0},{16,24},{24,16},{1,9},{9,1},{17,25},{25,17},{2,10},{10... | collective-permute-start | bytes 663560 | tf_op jit(solution)/shard_map/ppermute | solution.py:686
  7.1 0.7 %collective-permute-start.3 = (f32[6,72,128]{2,1,0:T(8,128)S(1)}, f32[6,72,128]{2,1,0:T(8,128)S(1)}, u32[]{:S(2)}, u32[]{:S(2)}) collective-permute-start(f32[6,72,128]{2,1,0:T(8,128)S(1)} %get-tuple-element.25), channel_id=1, source_target_pairs={{8,16},{16,8},{9,17},{17,9},{10,18},{18,10},{11,19},{19,11},{12,20... | collective-permute-start | bytes 663560 | tf_op jit(solution)/shard_map/ppermute | solution.py:687
  7.8 0.1 collective-permute-start
  7.9 3.7 %collective-permute-start.1 = (f32[2,72,128]{2,1,0:T(8,128)S(1)}, f32[2,72,128]{2,1,0:T(8,128)S(1)}, u32[]{:S(2)}, u32[]{:S(2)}) collective-permute-start(f32[2,72,128]{2,1,0:T(8,128)S(1)} %get-tuple-element.23), channel_id=1, source_target_pairs={{0,7},{1,2},{2,1},{3,4},{4,3},{5,6},{6,5},{7,0},{8,15},{9,10},{10,... | collective-permute-start | bytes 221192 | tf_op jit(solution)/shard_map/ppermute | solution.py:689
  11.6 4.6 %all-to-all-start = ((f32[32,1,128]{2,1,0:T(1,128)}), f32[32,1,128]{2,1,0:T(1,128)S(1)}, u32[]{:S(2)}, u32[]{:S(2)}) async-start(f32[32,1,128]{2,1,0:T(1,128)} %bitcast.18), calls=%async_computation | async-start | bytes 32768 | tf_op jit(solution)/shard_map/all_to_all | solution.py:682
  16.2 3.5 %shard_map.139 = (f32[24,72,128]{2,1,0:T(8,128)S(1)}, bf16[400,128]{1,0:T(8,128)(2,1)S(1)}) custom-call(f32[24,72,128]{2,1,0:T(8,128)S(1)} %get-tuple-element.18.state_ref, f32[24,72,128]{2,1,0:T(8,128)S(1)} %get-tuple-element.19.carried_ref, bf16[256,768]{1,0:T(8,128)(2,1)} %constant.2.clone.weight_hbm, bf16[400,128]{1,0:T(8,128)(2,1)S(1)} %get-tuple-element.20.mat_ref), custom_call_target="tpu_custom_call" | custom-call | tf_op jit(solution)/shard_map/pallas_call | solution.py:603
  19.7 0.0 collective-permute-done.first_y
  19.7 0.0 collective-permute-done.1.second_y
  19.7 0.0 collective-permute-done.2.first_x
  19.7 0.0 collective-permute-done.3.second_x
  19.7 3.3 %shard_map.140.rate_ref = f32[24,72,128]{2,1,0:T(8,128)S(1)} custom-call(f32[24,72,128]{2,1,0:T(8,128)S(1)} %get-tuple-element.18.state_ref, f32[24,72,128]{2,1,0:T(8,128)S(1)} %get-tuple-element.19.carried_ref, bf16[400,128]{1,0:T(8,128)(2,1)S(1)} %get-tuple-element.21.mat_ref, f32[2,72,128]{2,1,0:T(8,128)S(1)} %collective-permute-done.first_y, ...), custom_call_target="tpu_custom_call" | custom-call | tf_op jit(solution)/shard_map/pallas_call | solution.py:603
  23.0 0.3 %all-to-all-done = f32[32,1,128]{2,1,0:T(1,128)S(1)} async-done(((f32[32,1,128]{2,1,0:T(1,128)}), f32[32,1,128]{2,1,0:T(1,128)S(1)}, u32[]{:S(2)}, u32[]{:S(2)}) %all-to-all-start) | async-done | bytes 16416 | tf_op jit(solution)/shard_map/all_to_all | solution.py:682
  23.3 1.2 %shard_map.141 = (f32[512,384]{1,0:T(8,128)}, f32[8,384]{1,0:T(8,128)}, f32[24,384]{1,0:T(8,128)}, f32[1,1]{1,0:T(1,128)}) custom-call(f32[24,72,128]{2,1,0:T(8,128)S(1)} %get-tuple-element.18.state_ref, f32[24,72,128]{2,1,0:T(8,128)S(1)} %shard_map.140.rate_ref, f32[32,128]{1,0:T(8,128)S(1)} %bitcast.14), custom_call_target="tpu_custom_call" | custom-call | tf_op jit(solution)/shard_map/pallas_call | solution.py:603
Async XLA Ops:
  4.1 15.6 %collective-permute-start.2 = (f32[6,72,128]{2,1,0:T(8,128)S(1)}, f32[6,72,128]{2,1,0:T(8,128)S(1)}, u32[]{:S(2)}, u32[]{:S(2)}) collective-permute-start(f32[6,72,128]{2,1,0:T(8,128)S(1)} %get-tuple-element.24), channel_id=1, source_target_pairs={{0,8},{8,0},{16,24},{24,16},{1,9},{9,1},{17,25},{25,17},{2,10},{10... | collective-permute-start | bytes 663560 | tf_op jit(solution)/shard_map/ppermute | solution.py:686
  7.1 12.6 %collective-permute-start.3 = (f32[6,72,128]{2,1,0:T(8,128)S(1)}, f32[6,72,128]{2,1,0:T(8,128)S(1)}, u32[]{:S(2)}, u32[]{:S(2)}) collective-permute-start(f32[6,72,128]{2,1,0:T(8,128)S(1)} %get-tuple-element.25), channel_id=1, source_target_pairs={{8,16},{16,8},{9,17},{17,9},{10,18},{18,10},{11,19},{19,11},{12,20... | collective-permute-start | bytes 663560 | tf_op jit(solution)/shard_map/ppermute | solution.py:687
  7.8 11.9 %collective-permute-start = (f32[2,72,128]{2,1,0:T(8,128)S(1)}, f32[2,72,128]{2,1,0:T(8,128)S(1)}, u32[]{:S(2)}, u32[]{:S(2)}) collective-permute-start(f32[2,72,128]{2,1,0:T(8,128)S(1)} %get-tuple-element.22), channel_id=1, source_target_pairs={{0,1},{1,0},{2,3},{3,2},{4,5},{5,4},{6,7},{7,6},{8,9},{9,8},{10,11... | collective-permute-start | bytes 221192 | tf_op jit(solution)/shard_map/ppermute | solution.py:688
  7.9 11.8 %collective-permute-start.1 = (f32[2,72,128]{2,1,0:T(8,128)S(1)}, f32[2,72,128]{2,1,0:T(8,128)S(1)}, u32[]{:S(2)}, u32[]{:S(2)}) collective-permute-start(f32[2,72,128]{2,1,0:T(8,128)S(1)} %get-tuple-element.23), channel_id=1, source_target_pairs={{0,7},{1,2},{2,1},{3,4},{4,3},{5,6},{6,5},{7,0},{8,15},{9,10},{10,... | collective-permute-start | bytes 221192 | tf_op jit(solution)/shard_map/ppermute | solution.py:689
  11.6 11.7 %all-to-all-start = ((f32[32,1,128]{2,1,0:T(1,128)}), f32[32,1,128]{2,1,0:T(1,128)S(1)}, u32[]{:S(2)}, u32[]{:S(2)}) async-start(f32[32,1,128]{2,1,0:T(1,128)} %bitcast.18), calls=%async_computation | async-start | bytes 32768 | tf_op jit(solution)/shard_map/all_to_all | solution.py:682

commit v5 on v4

--- a/solution.py
+++ b/solution.py
@@ -86,10 +86,10 @@
         stacked = jnp.concatenate([high, high, low, low], axis=0)
         both = jnp.concatenate([mat_ref[...], mat_ref[...]], axis=1)
         product = jnp.dot(both, stacked, preferred_element_type=F32)
-        for i, (m, temper) in enumerate(pieces):
+        for i, (m, temper, *logs) in enumerate(pieces):
             part = product[:, i * LANES : (i + 1) * LANES]
             u = j * group + i if unit is None else unit(j, i)
-            logt = jnp.log(temper)
+            logt = logs[0] if logs else jnp.log(temper)
             total = part[(terms - 1) * species : terms * species]
             for k in range(terms - 2, -1, -1):
                 total = total * logt + part[k * species : (k + 1) * species]
@@ -195,30 +195,17 @@
     return out
 
 
-def cell_copies(conc_hbm, temper_hbm, motion_hbm, base_ref, sem):
-    copies = []
-    for t in range(base_ref.shape[0]):
-        start = 0
-        for k, src in enumerate((conc_hbm, temper_hbm, motion_hbm)):
-            dst = base_ref.at[t, pl.ds(start, src.shape[0])]
-            part = src.at[:, pl.ds(t * LANES, LANES)]
-            copies.append(pltpu.make_async_copy(part, dst, sem.at[3 * t + k]))
-            start += src.shape[0]
-    return copies
-
-
 def mixture_kernel(
     conc_hbm, temper_hbm, motion_hbm, mass_hbm, size_hbm, energy_hbm, poly_hbm, base_hbm,
     slope_hbm, crit_hbm,
     state_ref, carried_ref, mat_ref, first_x, second_x, first_y, second_y, rate_hbm,
-    rate_ref, base_ref, mass_ref, size_ref, energy_ref, poly_ref, heat_ref, slope_ref, crit_ref, lin_ref, plane_ref,
+    rate_ref, base_ref, temper_ref, motion_ref, log_ref, mass_ref, size_ref, energy_ref, poly_ref, heat_ref, slope_ref, crit_ref, lin_ref, plane_ref,
     table_sem, cell_sem, rate_sem,
 ):
     tiles = base_ref.shape[0]
     width = temper_hbm.shape[0]
     species = mass_ref.shape[1]
     units = tiles * width
-    cells = species * width
     pairs = (
         (mass_hbm, mass_ref), (size_hbm, size_ref), (energy_hbm, energy_ref),
         (poly_hbm, poly_ref), (base_hbm, heat_ref), (slope_hbm, slope_ref), (crit_hbm, crit_ref),
@@ -226,7 +213,14 @@
     tables = [
         pltpu.make_async_copy(src, dst, table_sem.at[k]) for k, (src, dst) in enumerate(pairs)
     ]
-    copies = cell_copies(conc_hbm, temper_hbm, motion_hbm, base_ref, cell_sem)
+    copies = [
+        pltpu.make_async_copy(
+            conc_hbm.at[:, pl.ds(t * LANES, LANES)], base_ref.at[t], cell_sem.at[t]
+        )
+        for t in range(tiles)
+    ]
+    for k, (src, dst) in enumerate(((temper_hbm, temper_ref), (motion_hbm, motion_ref))):
+        copies.append(pltpu.make_async_copy(src, dst, cell_sem.at[tiles + k]))
     for c in tables + copies:
         c.start()
     for c in tables:
@@ -237,17 +231,21 @@
     ids = row_ids()
 
     def ready(t):
-        for c in copies if t == 0 else ():
-            c.wait()
+        if t == 0:
+            for c in copies:
+                c.wait()
+            log_ref[...] = jnp.log(temper_ref[...])
 
     def read(t, x):
         mass = base_ref[t, pl.ds(x, species, stride=width), :]
-        return mass, base_ref[t, pl.ds(cells + x, 1), :]
+        ls = slice(t * LANES, (t + 1) * LANES)
+        return mass, temper_ref[x : x + 1, ls], log_ref[x : x + 1, ls]
 
     def extra(t, x, u, temper, density):
         block = jnp.where(ids == 0, temper, jnp.where(ids == 4, density, 0.0))
         for c in range(3):
-            row = base_ref[t, pl.ds(cells + (c + 1) * width + x, 1), :]
+            at = c * width + x
+            row = motion_ref[at : at + 1, t * LANES : (t + 1) * LANES]
             block = jnp.where(ids == c + 1, row, block)
         state_ref[u, species : species + EXTRA, :] = block
 
@@ -426,7 +424,8 @@
                 rate_ref[u] = rate_ref[u] + (fluxes[t] - back)
         return carry
 
-    lax.fori_loop(0, width // batch, work, 0)
+    for j in range(width // batch):
+        work(j, 0)
 
 
 def rim_kernel(
@@ -636,7 +635,6 @@
     conc = component_concentration.reshape(species * width, line)
     motion = motion_vector.reshape(3 * width, line)
     mat_rows = (terms + 2) * species + 16
-    count = (species + 4) * width
     keep = True
     field = ((units, rows, LANES), F32, keep)
     mix_scratch = lambda n: [pltpu.VMEM((n * 8, LANES), F32), pltpu.VMEM((5, n, LANES), F32)]
@@ -655,7 +653,10 @@
         [pl.ANY] * 10,
         [
             pltpu.VMEM((devices, LANES), F32),
-            pltpu.VMEM((tiles, count, LANES), F32),
+            pltpu.VMEM((tiles, species * width, LANES), F32),
+            pltpu.VMEM((width, line), F32),
+            pltpu.VMEM((3 * width, line), F32),
+            pltpu.VMEM((width, line), F32),
             pltpu.VMEM((1, species), F32),
             pltpu.VMEM((species, species), F32),
             pltpu.VMEM((species, species), F32),
@@ -665,7 +666,7 @@
             pltpu.VMEM((1, species), F32),
         ]
         + mix_scratch(units)
-        + [pltpu.SemaphoreType.DMA((7,)), pltpu.SemaphoreType.DMA((3 * tiles,))]
+        + [pltpu.SemaphoreType.DMA((7,)), pltpu.SemaphoreType.DMA((tiles + 2,))]
         + [pltpu.SemaphoreType.DMA(())],
     )(
         conc,

time: 24.7 us -> 24.5 us (level)
  Pallas kernels: 11.4 us -> 10.3 us
  waiting for transfers between devices: 0.27 us -> 1.25 us
    pallas_call x4, Pallas kernels: 11.4 us -> 10.3 us  [apply(): run(*[a if m is None else pltpu.with_memory_space_constraint(a, pltpu.VME...]
    all_to_all x1, waiting for transfers between devices: 0.26 us -> 1.24 us  [body(): top = lax.all_to_all(rate, ('gx', 'gy'), 0, 0, tiled=True)]
  transfers between devices with their start and end apart: 5 -> 5, of which waited for: 1 -> 1; matrix products, arithmetic and copies ran while one was open for 0% -> 0% of each run, Pallas kernels for 28% -> 24%
where the time goes in v5:
time: 24.5 us; the launch traced here: 24.3 us
  starting transfers between devices  12 us (49%)
  Pallas kernels  10.3 us (42%)
  waiting for transfers between devices  1.25 us (5%)
  between operations  0.72 us (3%)
    pallas_call x4, Pallas kernels, apply(): run(*[a if m is None else pltpu.with_memory_space_constraint(a, pltpu.VME...  10.3 us
    all_to_all x1, starting transfers between devices, body(): top = lax.all_to_all(rate, ('gx', 'gy'), 0, 0, tiled=True)  4.58 us
    ppermute x1, starting transfers between devices, body(): got_second_y = lax.ppermute(second_y, 'gy', pair_second(ny))  3.71 us
    ppermute x1, starting transfers between devices, body(): got_first_x = lax.ppermute(first_x, 'gx', pair_first(nx))  3.02 us
    all_to_all x1, waiting for transfers between devices, body(): top = lax.all_to_all(rate, ('gx', 'gy'), 0, 0, tiled=True)  1.24 us
    ppermute x1, starting transfers between devices, body(): got_second_x = lax.ppermute(second_x, 'gx', inside)  0.66 us
  transfers between devices with their start and end apart: 5, of which 1 were waited for; matrix products, arithmetic and copies ran while one was open for 0% of the time, Pallas kernels for 24%

profile of v5, /device:TPU:0, one launch (start us, length us, event | category | flops | bytes accessed | tf_op | source)
XLA Modules:
  0.0 24.3 jit_solution(13699383424333818712)
XLA Ops:
  0.6 3.3 %shard_map.138 = (f32[24,72,128]{2,1,0:T(8,128)S(1)}, f32[24,72,128]{2,1,0:T(8,128)S(1)}, bf16[400,128]{1,0:T(8,128)(2,1)S(1)}, f32[6,72,128]{2,1,0:T(8,128)S(1)...) custom-call(f32[512,384]{1,0:T(8,128)} %bitcast.15, ...), custom_call_target="tpu_custom_call" | custom-call | tf_op jit(solution)/shard_map/pallas_call | solution.py:602
  4.0 3.0 %collective-permute-start.2 = (f32[6,72,128]{2,1,0:T(8,128)S(1)}, f32[6,72,128]{2,1,0:T(8,128)S(1)}, u32[]{:S(2)}, u32[]{:S(2)}) collective-permute-start(f32[6,72,128]{2,1,0:T(8,128)S(1)} %get-tuple-element.24), channel_id=1, source_target_pairs={{0,8},{8,0},{16,24},{24,16},{1,9},{9,1},{17,25},{25,17},{2,10},{10... | collective-permute-start | bytes 663560 | tf_op jit(solution)/shard_map/ppermute | solution.py:687
  7.0 0.7 %collective-permute-start.3 = (f32[6,72,128]{2,1,0:T(8,128)S(1)}, f32[6,72,128]{2,1,0:T(8,128)S(1)}, u32[]{:S(2)}, u32[]{:S(2)}) collective-permute-start(f32[6,72,128]{2,1,0:T(8,128)S(1)} %get-tuple-element.25), channel_id=1, source_target_pairs={{8,16},{16,8},{9,17},{17,9},{10,18},{18,10},{11,19},{19,11},{12,20... | collective-permute-start | bytes 663560 | tf_op jit(solution)/shard_map/ppermute | solution.py:688
  7.6 0.1 collective-permute-start
  7.7 3.7 %collective-permute-start.1 = (f32[2,72,128]{2,1,0:T(8,128)S(1)}, f32[2,72,128]{2,1,0:T(8,128)S(1)}, u32[]{:S(2)}, u32[]{:S(2)}) collective-permute-start(f32[2,72,128]{2,1,0:T(8,128)S(1)} %get-tuple-element.23), channel_id=1, source_target_pairs={{0,7},{1,2},{2,1},{3,4},{4,3},{5,6},{6,5},{7,0},{8,15},{9,10},{10,... | collective-permute-start | bytes 221192 | tf_op jit(solution)/shard_map/ppermute | solution.py:690
  11.4 4.6 %all-to-all-start = ((f32[32,1,128]{2,1,0:T(1,128)}), f32[32,1,128]{2,1,0:T(1,128)S(1)}, u32[]{:S(2)}, u32[]{:S(2)}) async-start(f32[32,1,128]{2,1,0:T(1,128)} %bitcast.18), calls=%async_computation | async-start | bytes 32768 | tf_op jit(solution)/shard_map/all_to_all | solution.py:683
  16.0 2.5 %shard_map.139 = (f32[24,72,128]{2,1,0:T(8,128)S(1)}, bf16[400,128]{1,0:T(8,128)(2,1)S(1)}) custom-call(f32[24,72,128]{2,1,0:T(8,128)S(1)} %get-tuple-element.18.state_ref, f32[24,72,128]{2,1,0:T(8,128)S(1)} %get-tuple-element.19.carried_ref, bf16[256,768]{1,0:T(8,128)(2,1)} %constant.2.clone.weight_hbm, bf16[400,128]{1,0:T(8,128)(2,1)S(1)} %get-tuple-element.20.mat_ref), custom_call_target="tpu_custom_call" | custom-call | tf_op jit(solution)/shard_map/pallas_call | solution.py:602
  18.6 0.0 collective-permute-done.first_y
  18.6 0.0 collective-permute-done.1.second_y
  18.6 0.0 collective-permute-done.2.first_x
  18.6 0.0 collective-permute-done.3.second_x
  18.6 3.3 %shard_map.140.rate_ref = f32[24,72,128]{2,1,0:T(8,128)S(1)} custom-call(f32[24,72,128]{2,1,0:T(8,128)S(1)} %get-tuple-element.18.state_ref, f32[24,72,128]{2,1,0:T(8,128)S(1)} %get-tuple-element.19.carried_ref, bf16[400,128]{1,0:T(8,128)(2,1)S(1)} %get-tuple-element.21.mat_ref, f32[2,72,128]{2,1,0:T(8,128)S(1)} %collective-permute-done.first_y, ...), custom_call_target="tpu_custom_call" | custom-call | tf_op jit(solution)/shard_map/pallas_call | solution.py:602
  21.9 1.2 %all-to-all-done = f32[32,1,128]{2,1,0:T(1,128)S(1)} async-done(((f32[32,1,128]{2,1,0:T(1,128)}), f32[32,1,128]{2,1,0:T(1,128)S(1)}, u32[]{:S(2)}, u32[]{:S(2)}) %all-to-all-start) | async-done | bytes 16416 | tf_op jit(solution)/shard_map/all_to_all | solution.py:683
  23.1 1.2 %shard_map.141 = (f32[512,384]{1,0:T(8,128)}, f32[8,384]{1,0:T(8,128)}, f32[24,384]{1,0:T(8,128)}, f32[1,1]{1,0:T(1,128)}) custom-call(f32[24,72,128]{2,1,0:T(8,128)S(1)} %get-tuple-element.18.state_ref, f32[24,72,128]{2,1,0:T(8,128)S(1)} %shard_map.140.rate_ref, f32[32,128]{1,0:T(8,128)S(1)} %bitcast.14), custom_call_target="tpu_custom_call" | custom-call | tf_op jit(solution)/shard_map/pallas_call | solution.py:602
Async XLA Ops:
  4.0 14.6 %collective-permute-start.2 = (f32[6,72,128]{2,1,0:T(8,128)S(1)}, f32[6,72,128]{2,1,0:T(8,128)S(1)}, u32[]{:S(2)}, u32[]{:S(2)}) collective-permute-start(f32[6,72,128]{2,1,0:T(8,128)S(1)} %get-tuple-element.24), channel_id=1, source_target_pairs={{0,8},{8,0},{16,24},{24,16},{1,9},{9,1},{17,25},{25,17},{2,10},{10... | collective-permute-start | bytes 663560 | tf_op jit(solution)/shard_map/ppermute | solution.py:687
  7.0 11.6 %collective-permute-start.3 = (f32[6,72,128]{2,1,0:T(8,128)S(1)}, f32[6,72,128]{2,1,0:T(8,128)S(1)}, u32[]{:S(2)}, u32[]{:S(2)}) collective-permute-start(f32[6,72,128]{2,1,0:T(8,128)S(1)} %get-tuple-element.25), channel_id=1, source_target_pairs={{8,16},{16,8},{9,17},{17,9},{10,18},{18,10},{11,19},{19,11},{12,20... | collective-permute-start | bytes 663560 | tf_op jit(solution)/shard_map/ppermute | solution.py:688
  7.6 10.9 %collective-permute-start = (f32[2,72,128]{2,1,0:T(8,128)S(1)}, f32[2,72,128]{2,1,0:T(8,128)S(1)}, u32[]{:S(2)}, u32[]{:S(2)}) collective-permute-start(f32[2,72,128]{2,1,0:T(8,128)S(1)} %get-tuple-element.22), channel_id=1, source_target_pairs={{0,1},{1,0},{2,3},{3,2},{4,5},{5,4},{6,7},{7,6},{8,9},{9,8},{10,11... | collective-permute-start | bytes 221192 | tf_op jit(solution)/shard_map/ppermute | solution.py:689
  7.7 10.9 %collective-permute-start.1 = (f32[2,72,128]{2,1,0:T(8,128)S(1)}, f32[2,72,128]{2,1,0:T(8,128)S(1)}, u32[]{:S(2)}, u32[]{:S(2)}) collective-permute-start(f32[2,72,128]{2,1,0:T(8,128)S(1)} %get-tuple-element.23), channel_id=1, source_target_pairs={{0,7},{1,2},{2,1},{3,4},{4,3},{5,6},{6,5},{7,0},{8,15},{9,10},{10,... | collective-permute-start | bytes 221192 | tf_op jit(solution)/shard_map/ppermute | solution.py:690
  11.4 11.7 %all-to-all-start = ((f32[32,1,128]{2,1,0:T(1,128)}), f32[32,1,128]{2,1,0:T(1,128)S(1)}, u32[]{:S(2)}, u32[]{:S(2)}) async-start(f32[32,1,128]{2,1,0:T(1,128)} %bitcast.18), calls=%async_computation | async-start | bytes 32768 | tf_op jit(solution)/shard_map/all_to_all | solution.py:683

commit v6 on v5

--- a/solution.py
+++ b/solution.py
@@ -198,9 +198,9 @@
 def mixture_kernel(
     conc_hbm, temper_hbm, motion_hbm, mass_hbm, size_hbm, energy_hbm, poly_hbm, base_hbm,
     slope_hbm, crit_hbm,
-    state_ref, carried_ref, mat_ref, first_x, second_x, first_y, second_y, rate_hbm,
-    rate_ref, base_ref, temper_ref, motion_ref, log_ref, mass_ref, size_ref, energy_ref, poly_ref, heat_ref, slope_ref, crit_ref, lin_ref, plane_ref,
-    table_sem, cell_sem, rate_sem,
+    state_ref, carried_ref, mat_ref, first_x, second_x, first_y, second_y, rate_ref,
+    base_ref, temper_ref, motion_ref, log_ref, mass_ref, size_ref, energy_ref, poly_ref, heat_ref, slope_ref, crit_ref, lin_ref, plane_ref,
+    table_sem, cell_sem,
 ):
     tiles = base_ref.shape[0]
     width = temper_hbm.shape[0]
@@ -273,8 +273,6 @@
         best = step(x, best)
     top = jnp.maximum(jnp.max(best), jnp.max(rates))
     rate_ref[...] = jnp.full(rate_ref.shape, top, F32)
-    send = pltpu.make_async_copy(rate_ref, rate_hbm, rate_sem)
-    send.start()
 
     even_x = lax.rem(lax.axis_index("gx"), 2) == 0
     upper = (width - 2) * tiles
@@ -291,7 +289,6 @@
         high = pack_cells(state_ref, g * per * tiles + tiles - 1, tiles, LANES - reach, per)
         first_y[g] = jnp.where(even_y, high, low)
         second_y[g] = jnp.where(even_y, low, high)
-    send.wait()
 
 
 def weigh(before, here, after, beyond):
@@ -648,11 +645,10 @@
             ((2 * tiles, rows, LANES), F32, keep),
             ((packs, rows, LANES), F32, keep),
             ((packs, rows, LANES), F32, keep),
-            ((devices, LANES), F32, pl.ANY),
+            ((devices, LANES), F32, True),
         ],
         [pl.ANY] * 10,
         [
-            pltpu.VMEM((devices, LANES), F32),
             pltpu.VMEM((tiles, species * width, LANES), F32),
             pltpu.VMEM((width, line), F32),
             pltpu.VMEM((3 * width, line), F32),
@@ -666,8 +662,7 @@
             pltpu.VMEM((1, species), F32),
         ]
         + mix_scratch(units)
-        + [pltpu.SemaphoreType.DMA((7,)), pltpu.SemaphoreType.DMA((tiles + 2,))]
-        + [pltpu.SemaphoreType.DMA(())],
+        + [pltpu.SemaphoreType.DMA((7,)), pltpu.SemaphoreType.DMA((tiles + 2,))],
     )(
         conc,
         thermal_level,

time: 24.5 us -> 24.5 us (level)
  no operation moved by 1% of the time
where the time goes in v6:
time: 24.5 us; the launch traced here: 24.3 us
  starting transfers between devices  12 us (49%)
  Pallas kernels  10.3 us (42%)
  waiting for transfers between devices  1.25 us (5%)
  between operations  0.72 us (3%)
    pallas_call x4, Pallas kernels, apply(): run(*[a if m is None else pltpu.with_memory_space_constraint(a, pltpu.VME...  10.3 us
    all_to_all x1, starting transfers between devices, body(): top = lax.all_to_all(rate, ('gx', 'gy'), 0, 0, tiled=True)  4.58 us
    ppermute x1, starting transfers between devices, body(): got_second_y = lax.ppermute(second_y, 'gy', pair_second(ny))  3.7 us
    ppermute x1, starting transfers between devices, body(): got_first_x = lax.ppermute(first_x, 'gx', pair_first(nx))  3.03 us
    all_to_all x1, waiting for transfers between devices, body(): top = lax.all_to_all(rate, ('gx', 'gy'), 0, 0, tiled=True)  1.24 us
    ppermute x1, starting transfers between devices, body(): got_second_x = lax.ppermute(second_x, 'gx', inside)  0.66 us
  transfers between devices with their start and end apart: 5, of which 1 were waited for; matrix products, arithmetic and copies ran while one was open for 0% of the time, Pallas kernels for 24%

profile of v6, /device:TPU:0, one launch (start us, length us, event | category | flops | bytes accessed | tf_op | source)
XLA Modules:
  0.0 24.3 jit_solution(581398867809139880)
XLA Ops:
  0.6 3.3 %shard_map.138 = (f32[24,72,128]{2,1,0:T(8,128)S(1)}, f32[24,72,128]{2,1,0:T(8,128)S(1)}, bf16[400,128]{1,0:T(8,128)(2,1)S(1)}, f32[6,72,128]{2,1,0:T(8,128)S(1)...) custom-call(f32[512,384]{1,0:T(8,128)} %bitcast.15, ...), custom_call_target="tpu_custom_call" | custom-call | tf_op jit(solution)/shard_map/pallas_call | solution.py:599
  3.9 3.0 %collective-permute-start.2 = (f32[6,72,128]{2,1,0:T(8,128)S(1)}, f32[6,72,128]{2,1,0:T(8,128)S(1)}, u32[]{:S(2)}, u32[]{:S(2)}) collective-permute-start(f32[6,72,128]{2,1,0:T(8,128)S(1)} %get-tuple-element.24), channel_id=1, source_target_pairs={{0,8},{8,0},{16,24},{24,16},{1,9},{9,1},{17,25},{25,17},{2,10},{10... | collective-permute-start | bytes 663560 | tf_op jit(solution)/shard_map/ppermute | solution.py:682
  7.0 0.7 %collective-permute-start.3 = (f32[6,72,128]{2,1,0:T(8,128)S(1)}, f32[6,72,128]{2,1,0:T(8,128)S(1)}, u32[]{:S(2)}, u32[]{:S(2)}) collective-permute-start(f32[6,72,128]{2,1,0:T(8,128)S(1)} %get-tuple-element.25), channel_id=1, source_target_pairs={{8,16},{16,8},{9,17},{17,9},{10,18},{18,10},{11,19},{19,11},{12,20... | collective-permute-start | bytes 663560 | tf_op jit(solution)/shard_map/ppermute | solution.py:683
  7.6 0.1 collective-permute-start
  7.7 3.7 %collective-permute-start.1 = (f32[2,72,128]{2,1,0:T(8,128)S(1)}, f32[2,72,128]{2,1,0:T(8,128)S(1)}, u32[]{:S(2)}, u32[]{:S(2)}) collective-permute-start(f32[2,72,128]{2,1,0:T(8,128)S(1)} %get-tuple-element.23), channel_id=1, source_target_pairs={{0,7},{1,2},{2,1},{3,4},{4,3},{5,6},{6,5},{7,0},{8,15},{9,10},{10,... | collective-permute-start | bytes 221192 | tf_op jit(solution)/shard_map/ppermute | solution.py:685
  11.4 4.6 %all-to-all-start = ((f32[32,1,128]{2,1,0:T(1,128)}), f32[32,1,128]{2,1,0:T(1,128)S(1)}, u32[]{:S(2)}, u32[]{:S(2)}) async-start(f32[32,1,128]{2,1,0:T(1,128)} %bitcast.8), calls=%async_computation | async-start | bytes 32768 | tf_op jit(solution)/shard_map/all_to_all | solution.py:678
  16.0 2.5 %shard_map.139 = (f32[24,72,128]{2,1,0:T(8,128)S(1)}, bf16[400,128]{1,0:T(8,128)(2,1)S(1)}) custom-call(f32[24,72,128]{2,1,0:T(8,128)S(1)} %get-tuple-element.18.state_ref, f32[24,72,128]{2,1,0:T(8,128)S(1)} %get-tuple-element.19.carried_ref, bf16[256,768]{1,0:T(8,128)(2,1)} %constant.2.clone.weight_hbm, bf16[400,128]{1,0:T(8,128)(2,1)S(1)} %get-tuple-element.20.mat_ref), custom_call_target="tpu_custom_call" | custom-call | tf_op jit(solution)/shard_map/pallas_call | solution.py:599
  18.6 0.0 collective-permute-done.first_y
  18.6 0.0 collective-permute-done.1.second_y
  18.6 0.0 collective-permute-done.2.first_x
  18.6 0.0 collective-permute-done.3.second_x
  18.6 3.3 %shard_map.140.rate_ref = f32[24,72,128]{2,1,0:T(8,128)S(1)} custom-call(f32[24,72,128]{2,1,0:T(8,128)S(1)} %get-tuple-element.18.state_ref, f32[24,72,128]{2,1,0:T(8,128)S(1)} %get-tuple-element.19.carried_ref, bf16[400,128]{1,0:T(8,128)(2,1)S(1)} %get-tuple-element.21.mat_ref, f32[2,72,128]{2,1,0:T(8,128)S(1)} %collective-permute-done.first_y, ...), custom_call_target="tpu_custom_call" | custom-call | tf_op jit(solution)/shard_map/pallas_call | solution.py:599
  21.9 1.2 %all-to-all-done = f32[32,1,128]{2,1,0:T(1,128)S(1)} async-done(((f32[32,1,128]{2,1,0:T(1,128)}), f32[32,1,128]{2,1,0:T(1,128)S(1)}, u32[]{:S(2)}, u32[]{:S(2)}) %all-to-all-start) | async-done | bytes 16416 | tf_op jit(solution)/shard_map/all_to_all | solution.py:678
  23.1 1.2 %shard_map.141 = (f32[512,384]{1,0:T(8,128)}, f32[8,384]{1,0:T(8,128)}, f32[24,384]{1,0:T(8,128)}, f32[1,1]{1,0:T(1,128)}) custom-call(f32[24,72,128]{2,1,0:T(8,128)S(1)} %get-tuple-element.18.state_ref, f32[24,72,128]{2,1,0:T(8,128)S(1)} %shard_map.140.rate_ref, f32[32,128]{1,0:T(8,128)S(1)} %bitcast.14), custom_call_target="tpu_custom_call" | custom-call | tf_op jit(solution)/shard_map/pallas_call | solution.py:599
Async XLA Ops:
  3.9 14.6 %collective-permute-start.2 = (f32[6,72,128]{2,1,0:T(8,128)S(1)}, f32[6,72,128]{2,1,0:T(8,128)S(1)}, u32[]{:S(2)}, u32[]{:S(2)}) collective-permute-start(f32[6,72,128]{2,1,0:T(8,128)S(1)} %get-tuple-element.24), channel_id=1, source_target_pairs={{0,8},{8,0},{16,24},{24,16},{1,9},{9,1},{17,25},{25,17},{2,10},{10... | collective-permute-start | bytes 663560 | tf_op jit(solution)/shard_map/ppermute | solution.py:682
  7.0 11.6 %collective-permute-start.3 = (f32[6,72,128]{2,1,0:T(8,128)S(1)}, f32[6,72,128]{2,1,0:T(8,128)S(1)}, u32[]{:S(2)}, u32[]{:S(2)}) collective-permute-start(f32[6,72,128]{2,1,0:T(8,128)S(1)} %get-tuple-element.25), channel_id=1, source_target_pairs={{8,16},{16,8},{9,17},{17,9},{10,18},{18,10},{11,19},{19,11},{12,20... | collective-permute-start | bytes 663560 | tf_op jit(solution)/shard_map/ppermute | solution.py:683
  7.6 10.9 %collective-permute-start = (f32[2,72,128]{2,1,0:T(8,128)S(1)}, f32[2,72,128]{2,1,0:T(8,128)S(1)}, u32[]{:S(2)}, u32[]{:S(2)}) collective-permute-start(f32[2,72,128]{2,1,0:T(8,128)S(1)} %get-tuple-element.22), channel_id=1, source_target_pairs={{0,1},{1,0},{2,3},{3,2},{4,5},{5,4},{6,7},{7,6},{8,9},{9,8},{10,11... | collective-permute-start | bytes 221192 | tf_op jit(solution)/shard_map/ppermute | solution.py:684
  7.7 10.9 %collective-permute-start.1 = (f32[2,72,128]{2,1,0:T(8,128)S(1)}, f32[2,72,128]{2,1,0:T(8,128)S(1)}, u32[]{:S(2)}, u32[]{:S(2)}) collective-permute-start(f32[2,72,128]{2,1,0:T(8,128)S(1)} %get-tuple-element.23), channel_id=1, source_target_pairs={{0,7},{1,2},{2,1},{3,4},{4,3},{5,6},{6,5},{7,0},{8,15},{9,10},{10,... | collective-permute-start | bytes 221192 | tf_op jit(solution)/shard_map/ppermute | solution.py:685
  11.4 11.7 %all-to-all-start = ((f32[32,1,128]{2,1,0:T(1,128)}), f32[32,1,128]{2,1,0:T(1,128)S(1)}, u32[]{:S(2)}, u32[]{:S(2)}) async-start(f32[32,1,128]{2,1,0:T(1,128)} %bitcast.8), calls=%async_computation | async-start | bytes 32768 | tf_op jit(solution)/shard_map/all_to_all | solution.py:678
